TPU v7x, 256 devices: a whole 4x4x8 slice. The times are simulated.
256 devices in a mesh: row: 8 (over y, x_lo), col: 32 (over z, x_hi, core).
Axes of the slice: x: 4 (x_hi: 2, x_lo: 2; x = x_hi * 2 + x_lo), y: 4, z: 8, core: 2. Of those that a mesh axis runs over, the one named last changes fastest.
Arguments:
- blocks: bfloat16 [32, 4096, 8192], P('row', 'col'), may hold values from -1800 to 1800, as said below
- factor_b: float32 [8192, 256], P('col'), may hold values from -6 to 6
- factor_c: float32 [64, 256], replicated, may hold values from -0.75 to 0.75
- block_pos: int32 [32, 32], P('row', 'col'), may hold values from 0 to 7, as said below
- block_count: int32 [8, 32], P('row', 'col'), may hold values from 1 to 4, as said below
Outputs:
- factor_a_new: float32 [4096, 256], P(('row', 'col'))
- factor_b_new: float32 [8192, 256], P(('col', 'row'))
Inputs may be any that keep to these rules, and one draw needn't show every extreme that they name: `blocks`: every entry is finite. `block_pos`: the 4 positions of one device are distinct. `block_count`: some device has all 4 slots live.
All inputs are finite; a program needn't handle non-finite values.
Results may differ from a plain program's by a relative error of at most 0.007.
Values may be sent and summed in bfloat16 or wider, within the bound.
A program may use at most 64 MiB of HBM per device.

v0:
```python
import jax
import jax.numpy as jnp
from jax import lax
from jax.sharding import PartitionSpec as P

IB_DEV = 4
JB_DEV = 2


norm_eps = 1e-06


def solve_right(rows_in, matrix):
    lower = jnp.linalg.cholesky(matrix)
    half = lax.linalg.triangular_solve(
        lower, rows_in, left_side=False, lower=True, transpose_a=True
    )
    return lax.linalg.triangular_solve(lower, half, left_side=False, lower=True, transpose_a=False)


def body(blocks, factor_b, factor_c, block_pos, block_count):
    high = lax.Precision.HIGHEST
    tile_side = blocks.shape[1]
    depth = factor_c.shape[0]
    rank_width = factor_c.shape[1]
    col_slab = factor_b.shape[0]
    row_slab = IB_DEV * tile_side
    live_count = block_count[0, 0]
    positions = block_pos[:, 0]
    c_low = factor_c.astype(jnp.bfloat16)
    b_low = factor_b.astype(jnp.bfloat16)
    gram_c = jnp.dot(factor_c.T, factor_c, precision=high)
    gram_b = lax.psum(jnp.dot(factor_b.T, factor_b, precision=high), "col")
    v_one = gram_b * gram_c

    def cube_of(index):
        tile = lax.dynamic_index_in_dim(blocks, index, 0, keepdims=False)
        return tile.reshape(tile_side, tile_side, depth)

    def first_term(cube, b_tile):
        inner = lax.dot_general(
            cube, c_low, (((2,), (0,)), ((), ())), preferred_element_type=jnp.float32
        )
        return jnp.sum(inner * b_tile.astype(jnp.float32)[None], axis=1)

    def second_term(cube, a_tile):
        inner = lax.dot_general(
            cube, c_low, (((2,), (0,)), ((), ())), preferred_element_type=jnp.float32
        )
        return jnp.sum(inner * a_tile.astype(jnp.float32)[:, None, :], axis=0)

    def mode_one(index, total):
        place = positions[index]
        b_tile = lax.dynamic_slice_in_dim(b_low, place % JB_DEV * tile_side, tile_side, 0)
        term = first_term(cube_of(index), b_tile)
        start = place // JB_DEV * tile_side
        old = lax.dynamic_slice_in_dim(total, start, tile_side, 0)
        return lax.dynamic_update_slice_in_dim(total, old + term, start, 0)

    partial_a = lax.fori_loop(
        0, live_count, mode_one, jnp.zeros((row_slab, rank_width), jnp.float32)
    )
    rows_total = row_slab * lax.axis_size("row")
    share_rows = row_slab // lax.axis_size("col")
    sum_a = lax.psum(partial_a, "col")
    new_full = solve_right(sum_a, v_one)
    gram_a = lax.psum(jnp.dot(new_full.T, new_full, precision=high), "row")
    scale_a = jnp.sqrt(jnp.diagonal(gram_a) / rows_total + norm_eps)
    hat_full = new_full / scale_a[None, :]
    slab_low = hat_full.astype(jnp.bfloat16)
    hat_a = lax.dynamic_slice_in_dim(hat_full, lax.axis_index("col") * share_rows, share_rows, 0)
    v_two = gram_a / (scale_a[:, None] * scale_a[None, :]) * gram_c

    def mode_two(index, total):
        place = positions[index]
        a_tile = lax.dynamic_slice_in_dim(slab_low, place // JB_DEV * tile_side, tile_side, 0)
        term = second_term(cube_of(index), a_tile)
        start = place % JB_DEV * tile_side
        old = lax.dynamic_slice_in_dim(total, start, tile_side, 0)
        return lax.dynamic_update_slice_in_dim(total, old + term, start, 0)

    partial_b = lax.fori_loop(
        0, live_count, mode_two, jnp.zeros((col_slab, rank_width), jnp.float32)
    )
    part_b = lax.psum_scatter(partial_b, "row", scatter_dimension=0, tiled=True)
    new_b = solve_right(part_b, v_two)
    squares_b = lax.psum(jnp.sum(new_b * new_b, axis=0), ("row", "col"))
    scale_b = jnp.sqrt(squares_b / (col_slab * lax.axis_size("col")) + norm_eps)
    hat_b = new_b / scale_b[None, :]
    return (hat_a, hat_b)


def solution(mesh):
    return jax.shard_map(
        body,
        mesh=mesh,
        in_specs=(P("row", "col", None), P("col", None), P(), P("row", "col"), P("row", "col")),
        out_specs=(P(("row", "col"), None), P(("col", "row"), None)),
        check_vma=False,
    )
```

profile of v0, /device:TPU:1, one launch (start us, length us, event | category | flops | bytes accessed | tf_op | source)
XLA Modules:
  0.0 711.8 jit_solution(14343702082353428203)
XLA Ops:
  8.2 2.3 fusion.33
  10.5 12.0 %copy.17 = bf16[4,128,8192]{1,2,0:T(8,128)(2,1)} copy(bf16[4,128,8192]{2,1,0:T(8,128)(2,1)} %param.10) | data formatting | bytes 16777216 | tf_op jit(solution)/shard_map/while | solution.py:60
  22.6 13.4 %while.26 = (s32[]{:T(128)}, f32[512,256]{1,0:T(8,128)S(1)}, s32[]{:T(128)}, s32[4]{0:T(128)S(1)}, bf16[4,128,8192]{1,2,0:T(8,128)(2,1)}, /*index=5*/bf16[64,256...) while((s32[]{:T(128)}, f32[512,256]{1,0:T(8,128)S(1)}, ...), condition=%wide.region_2.3_spmd, body=%wide.region_0.2_spmd.sunk | while | flops 545292288 | bytes 11370982 | solution.py:60
  26.1 1.7 constant_dynamic-slice_fusion.11
  27.8 3.5 copy.34
  31.3 4.0 multiply_reduce_fusion.5
  37.1 313.5 %all-reduce.7.cloned.1.call-done = (f32[512,256]{1,0:T(8,128)}, f32[256,256]{0,1:T(8,128)}) async-done(((f32[512,256]{1,0:T(8,128)}, f32[256,256]{0,1:T(8,128)}), (f32[512,256]{1,0:T(8,128)}, f32[256,256]{0,1:T(8,128)})) %all-reduce.7.cloned.1.call-update) | async-done | bytes 786448 | tf_op jit(solution)/shard_map/psum | solution.py:65
  352.2 11.7 %cholesky.130 = f32[128,128]{1,0:T(8,128)S(1)} custom-call(f32[128,128]{1,0:T(8,128)S(1)} %cholesky.194), custom_call_target="Cholesky" | custom-call | tf_op jit(solution)/shard_map/jit(cholesky)/cholesky | solution.py:14
  364.0 9.8 %custom-call.23 = f32[1,128,128]{1,2,0:T(8,128)S(1)} custom-call(f32[1,128,128]{2,1,0:T(8,128)S(1)} %get-tuple-element.295), custom_call_target="InvertDiagBlocksLowerTriangular" | custom-call | tf_op jit(solution)/shard_map/jit(cholesky)/cholesky | solution.py:14
  374.3 11.7 %cholesky.147 = f32[128,128]{1,0:T(8,128)S(1)} custom-call(f32[128,128]{1,0:T(8,128)S(1)} %convolution_subtract_fusion.3), custom_call_target="Cholesky" | custom-call | tf_op jit(solution)/shard_map/jit(cholesky)/cholesky | solution.py:14
  388.1 4.2 while.28
  392.3 19.7 %custom-call.18 = f32[2,128,128]{1,2,0:T(8,128)S(1)} custom-call(f32[2,128,128]{2,1,0:T(8,128)S(1)} %get-tuple-element.202), custom_call_target="InvertDiagBlocksLowerTriangular" | custom-call | tf_op jit(solution)/shard_map/triangular_solve | solution.py:15
  416.0 73.3 %all-reduce.5.cloned.1.call-done = f32[256,256]{0,1:T(8,128)} async-done(((f32[256,256]{0,1:T(8,128)}), f32[256,256]{0,1:T(8,128)}) %all-reduce.5.cloned.1.call-update) | async-done | bytes 262160 | tf_op jit(solution)/shard_map/psum | solution.py:67
  489.2 2.7 gather_fusion
  493.2 11.7 %cholesky.164 = f32[128,128]{1,0:T(8,128)S(1)} custom-call(f32[128,128]{1,0:T(8,128)S(1)} %cholesky.197), custom_call_target="Cholesky" | custom-call | tf_op jit(solution)/shard_map/jit(cholesky)/cholesky | solution.py:14
  504.9 9.8 %custom-call.24 = f32[1,128,128]{1,2,0:T(8,128)S(1)} custom-call(f32[1,128,128]{2,1,0:T(8,128)S(1)} %get-tuple-element.291), custom_call_target="InvertDiagBlocksLowerTriangular" | custom-call | tf_op jit(solution)/shard_map/jit(cholesky)/cholesky | solution.py:14
  515.2 11.7 %cholesky.181 = f32[128,128]{1,0:T(8,128)S(1)} custom-call(f32[128,128]{1,0:T(8,128)S(1)} %convolution_subtract_fusion.2), custom_call_target="Cholesky" | custom-call | tf_op jit(solution)/shard_map/jit(cholesky)/cholesky | solution.py:14
  528.3 14.7 %while.27 = (s32[]{:T(128)}, f32[256,256]{1,0:T(8,128)S(1)}, s32[]{:T(128)}, s32[4]{0:T(128)S(1)}, bf16[4,128,8192]{1,2,0:T(8,128)(2,1)}, /*index=5*/bf16[64,256...) while((s32[]{:T(128)}, f32[256,256]{1,0:T(8,128)S(1)}, ...), condition=%wide.region_12.14_spmd, body=%wide.region_10.13_spmd.sunk | while | flops 545292288 | bytes 11633126 | solution.py:82
  533.4 3.5 copy.35
  537.7 4.6 multiply_reduce_fusion.6
  545.0 3.9 while.29
  548.9 19.7 %custom-call.19 = f32[2,128,128]{1,2,0:T(8,128)S(1)} custom-call(f32[2,128,128]{2,1,0:T(8,128)S(1)} %get-tuple-element.210), custom_call_target="InvertDiagBlocksLowerTriangular" | custom-call | tf_op jit(solution)/shard_map/triangular_solve | solution.py:15
  568.6 54.3 %reduce-scatter.2.cloned.1.call-done = f32[32,256]{1,0:T(8,128)} async-done(((f32[256,256]{1,0:T(8,128)}), f32[32,256]{1,0:T(8,128)}) %reduce-scatter.2.cloned.1.call-update) | async-done | bytes 32784 | tf_op jit(solution)/shard_map/reduce_scatter | solution.py:85
  625.5 78.7 %psum.31 = f32[256]{0:T(256)S(1)} all-reduce(f32[256]{0:T(256)S(1)} %multiply_reduce_fusion.2), channel_id=1, replica_groups=mesh['row'=8,'col'=32] {'row','col'}, use_global_device_ids=true, to_apply=%region_15.17 | all-reduce | flops 256 | bytes 2048 | tf_op jit(solution)/shard_map/psum | solution.py:87
  (91 shorter events, 26.9 us)
Async XLA Ops:
  7.2 343.5 %all-reduce.7.cloned.1.call-start = ((), (), s32[]{:S(2)}) async-start(), calls=%async_computation.3 | async-start | bytes 1572864 | tf_op jit(solution)/shard_map/psum | solution.py:65
  10.5 12.0 %copy-start.3 = (f32[64,256]{1,0:T(8,128)S(1)}, f32[64,256]{1,0:T(8,128)}, u32[]{:S(2)}) copy-start(f32[64,256]{1,0:T(8,128)} %param.12) | copy-start | bytes 196612
  10.5 12.0 %copy-start.5 = (s32[4,1]{0,1:T(1,128)S(1)}, s32[4,1]{0,1:T(1,128)}, u32[]{:S(2)}) copy-start(s32[4,1]{0,1:T(1,128)} %param.13) | copy-start | bytes 52
  36.0 0.9 copy-start.1
  36.9 452.3 %all-reduce.5.cloned.1.call-start = ((), (), s32[]{:S(2)}) async-start(), calls=%async_computation.1 | async-start | bytes 524288 | tf_op jit(solution)/shard_map/psum | solution.py:67
  352.0 60.0 %copy-start.4 = (f32[512,256]{1,0:T(8,128)S(1)}, f32[512,256]{1,0:T(8,128)}, u32[]{:S(2)}) copy-start(f32[512,256]{1,0:T(8,128)} %get-tuple-element.280) | copy-start | bytes 1572868
  415.9 207.0 %reduce-scatter.2.cloned.1.call-start = ((), (), s32[]{:S(2)}) async-start(), calls=%async_computation.2 | async-start | bytes 294912 | tf_op jit(solution)/shard_map/reduce_scatter | solution.py:85
  489.2 3.6 copy-start
  543.0 0.7 copy-start.2
Sparse Core Ops, SparseCore 0:
  37.0 313.5 all-reduce.6
  416.0 73.1 all-reduce.4
  543.9 78.9 reduce-scatter.1
where the time goes:
time: 724 us; the launch traced here: 712 us
  waiting for transfers between devices  441 us (61%)
  other arithmetic  110 us (15%)
  blocking collectives  78.7 us (11%)
  local copies, waits for them, and re-layouts  36.9 us (5%)
  matrix products  19.6 us (3%)
  between operations  17.1 us (2%)
  loops' own time  8.05 us (1%)
    psum x1, waiting for transfers between devices, body(): sum_a = lax.psum(partial_a, 'col')  314 us
    psum x1, blocking collectives, body(): squares_b = lax.psum(jnp.sum(new_b * new_b, axis=0), ('row', 'col'))  78.7 us
    psum x1, waiting for transfers between devices, body(): gram_a = lax.psum(jnp.dot(new_full.T, new_full, precision=high), 'row')  73.3 us
    another operation x13, other arithmetic, solve_right(): lower = jnp.linalg.cholesky(matrix)  68.6 us
    reduce_scatter x1, waiting for transfers between devices, body(): part_b = lax.psum_scatter(partial_b, 'row', scatter_dimension=0, tiled=True)  54.3 us
    another operation x5, other arithmetic, solve_right(): lax.linalg.triangular_solve(lower, rows_in, left_side=False, lower=True,...  39.4 us
  transfers between devices with their start and end apart: 3, of which 3 were waited for; matrix products, arithmetic and copies ran while one was open for 3% of the time, Pallas kernels for 0%

commit v1 on v0

v1 whole, which is shorter than its diff:
```python
import functools

import jax
import jax.numpy as jnp
from jax import lax
from jax.experimental import pallas as pl
from jax.experimental.pallas import tpu as pltpu
from jax.sharding import PartitionSpec as P

MESH = pl.DeviceIdType.MESH
HIGH = lax.Precision.HIGHEST
F32 = jnp.float32
BF16 = jnp.bfloat16
NROW, NCOL = 8, 32
R, K, BLK, SLOTS, IBD, JBD = 256, 64, 128, 4, 4, 2
SLAB_A = IBD * BLK
SLAB_B = JBD * BLK
WIDE = BLK * K
CHUNK = 1024
NCH = WIDE // CHUNK
JPC = CHUNK // K
SHARE_A = SLAB_A // NCOL
SHARE_B = SLAB_B // NROW
ROWS_A = SLAB_A * NROW
ROWS_B = SLAB_B * NCOL
EPS = 1e-06
MAX_IT = 80


def dot_hi(a, b):
    return jnp.dot(a, b, precision=HIGH, preferred_element_type=F32)


def wait_bytes(ref, sem):
    pltpu.make_async_copy(ref, ref, sem).wait()


def greet(axes):
    barrier = pltpu.get_barrier_semaphore()
    total = 0
    for axis, count in axes:
        me = lax.axis_index(axis)

        def one(k, carry, axis=axis, count=count, me=me):
            pl.semaphore_signal(
                barrier, inc=1, device_id={axis: lax.rem(me + k, count)}, device_id_type=MESH
            )
            return carry

        lax.fori_loop(1, count, one, 0)
        total += count - 1
    return barrier, total


def scatter(axis, count, src, dst, send, recv):
    me = lax.axis_index(axis)

    def one(k, carry):
        d = lax.rem(me + k, count)
        pltpu.make_async_remote_copy(
            src_ref=src.at[d], dst_ref=dst.at[k - 1], send_sem=send, recv_sem=recv,
            device_id={axis: d}, device_id_type=MESH,
        ).start()
        return carry

    lax.fori_loop(1, count, one, 0)


def gather(axis, count, piece, send, recv):
    me = lax.axis_index(axis)

    def one(k, carry):
        pltpu.make_async_remote_copy(
            src_ref=piece, dst_ref=piece, send_sem=send, recv_sem=recv,
            device_id={axis: lax.rem(me + k, count)}, device_id_type=MESH,
        ).start()
        return carry

    lax.fori_loop(1, count, one, 0)


def spread(axis, count, src, dst, send, recv):
    me = lax.axis_index(axis)

    def one(k, carry):
        pltpu.make_async_remote_copy(
            src_ref=src, dst_ref=dst.at[k - 1], send_sem=send, recv_sem=recv,
            device_id={axis: lax.rem(me + k, count)}, device_id_type=MESH,
        ).start()
        return carry

    lax.fori_loop(1, count, one, 0)


def kernel_a(
    pos, cnt, x_hbm, b_ref, c_ref,
    gb_out, m16_out, ms_out, g_out,
    x_v, x_sem, br, w_v, acc,
    gram, gb_part, gb_recv, gb_col, gb_full,
    part, m_recv, ms, g_recv, g_piece, g_full,
    send, recv,
):
    me_r, me_c = lax.axis_index("row"), lax.axis_index("col")

    def x_copy(ch):
        cols = pl.ds(pl.multiple_of(ch * CHUNK, CHUNK), CHUNK)
        return pltpu.make_async_copy(x_hbm.at[:, cols], x_v.at[:, cols], x_sem.at[ch])

    for ch in range(NCH):
        x_copy(ch).start()
    barrier, partners = greet((("col", NCOL), ("row", NROW)))

    b = b_ref[...]
    gram[...] = dot_hi(b.T, b)
    rows = gram[pl.ds(pl.multiple_of(me_r * 32, 32), 32), :]
    for i in range(32):
        gb_part[i] = rows[i:i + 1, :]
    br[...] = b.astype(BF16).astype(F32)
    cr = c_ref[...].astype(BF16).astype(F32)
    acc[...] = jnp.zeros_like(acc)

    def mode_one(ch, carry):
        for jb in range(JBD):
            tile = br[pl.ds(pl.multiple_of(jb * BLK + ch * JPC, JPC), JPC), :]
            for j in range(JPC):
                w_v[j * K:(j + 1) * K, jb * R:(jb + 1) * R] = (tile[j:j + 1, :] * cr).astype(BF16)
        x_copy(ch).wait()
        x = x_v[:, pl.ds(pl.multiple_of(ch * CHUNK, CHUNK), CHUNK)]
        acc[...] += jnp.dot(x, w_v[...], preferred_element_type=F32)
        return carry

    lax.fori_loop(0, NCH, mode_one, 0)
    count = cnt[0, 0]
    for ib in range(IBD):
        total = jnp.zeros((BLK, R), F32)
        for s in range(SLOTS):
            p = pos[s, 0]
            live = jnp.where(count > s, 1.0, 0.0).astype(F32)
            for jb in range(JBD):
                keep = jnp.where(p == ib * JBD + jb, live, 0.0)
                total += acc[s * BLK:(s + 1) * BLK, jb * R:(jb + 1) * R] * keep
        low = total.astype(BF16)
        for t in range(BLK // SHARE_A):
            part[ib * (BLK // SHARE_A) + t] = low[t * SHARE_A:(t + 1) * SHARE_A, :]

    pl.semaphore_wait(barrier, partners)
    scatter("col", NCOL, gb_part, gb_recv, send.at[0], recv.at[0])
    scatter("col", NCOL, part, m_recv, send.at[1], recv.at[1])

    wait_bytes(gb_recv, recv.at[0])
    gb_col[me_c] = gb_part[me_c] + jnp.sum(gb_recv[...], axis=0)
    gather("col", NCOL, gb_col.at[me_c], send.at[2], recv.at[2])

    wait_bytes(m_recv, recv.at[1])
    m16 = part[me_c].astype(F32) + jnp.sum(m_recv[...].astype(F32), axis=0)
    m16_out[...] = m16
    ms[me_c] = m16.astype(BF16)
    gather("col", NCOL, ms.at[me_c], send.at[3], recv.at[3])

    wait_bytes(gb_col.at[pl.ds(0, NCOL - 1)], recv.at[2])
    for i in range(32):
        gb_full[me_r, i:i + 1, :] = gb_col[i]
    gather("row", NROW, gb_full.at[me_r], send.at[4], recv.at[4])

    wait_bytes(ms.at[pl.ds(0, NCOL - 1)], recv.at[3])
    slab = ms[...].reshape(SLAB_A, R)
    ms_out[...] = slab
    gram[...] = jnp.dot(slab.T, slab, preferred_element_type=F32)
    g_piece[...] = gram[pl.ds(pl.multiple_of(me_c * 8, 8), 8), :]
    spread("row", NROW, g_piece, g_recv, send.at[5], recv.at[5])

    wait_bytes(gb_full.at[pl.ds(0, NROW - 1)], recv.at[4])
    gb_out[...] = gb_full[...].reshape(R, R)

    wait_bytes(g_recv, recv.at[5])
    g_full[me_c] = g_piece[...] + jnp.sum(g_recv[...], axis=0)
    gather("col", NCOL, g_full.at[me_c], send.at[6], recv.at[6])
    wait_bytes(g_full.at[pl.ds(0, NCOL - 1)], recv.at[6])
    g_out[...] = g_full[...].reshape(R, R)

    wait_bytes(gb_recv, send.at[0])
    wait_bytes(m_recv, send.at[1])
    wait_bytes(gb_col.at[pl.ds(0, NCOL - 1)], send.at[2])
    wait_bytes(ms.at[pl.ds(0, NCOL - 1)], send.at[3])
    wait_bytes(gb_full.at[pl.ds(0, NROW - 1)], send.at[4])
    wait_bytes(g_recv, send.at[5])
    wait_bytes(g_full.at[pl.ds(0, NCOL - 1)], send.at[6])


def eye():
    return lax.broadcasted_iota(jnp.int32, (R, R), 0) == lax.broadcasted_iota(jnp.int32, (R, R), 1)


def diagonals(v):
    only = jnp.where(eye(), v, 0.0)
    return jnp.sum(only, axis=1, keepdims=True), jnp.sum(only, axis=0, keepdims=True)


def inverse(v, x_ref, r_ref, c_ref):
    down, across = diagonals(v)
    down, across = 1.0 / jnp.sqrt(down), 1.0 / jnp.sqrt(across)
    unit = jnp.where(eye(), 1.0, 0.0)
    c = v * down * across
    c_ref[...] = c
    norm = jnp.max(jnp.sum(jnp.abs(c), axis=1, keepdims=True))
    alpha = jnp.where(norm < 1.9, 1.0, 1.0 / norm)
    res = unit - alpha * c
    x_ref[...] = alpha * (unit + res)
    res = unit - dot_hi(c, x_ref[...])
    r_ref[...] = res

    def more(state):
        it, size, before = state
        return (it < MAX_IT) & (size > 1e-5) & ((size > 1e-3) | (size < 0.5 * before))

    def step(state):
        it, size, _ = state
        x = x_ref[...]
        x = x + dot_hi(x, r_ref[...])
        x_ref[...] = x
        res = unit - dot_hi(c_ref[...], x)
        r_ref[...] = res
        return it + 1, jnp.max(jnp.abs(res)), size

    lax.while_loop(more, step, (0, jnp.max(jnp.abs(res)), jnp.float32(1e30)))
    x = x_ref[...]
    x = x + dot_hi(x, r_ref[...])
    return x * down * across


def kernel_b(
    pos, cnt, x_hbm, c_ref, gb_ref, m16_ref, ms_ref, g_ref,
    a_out, pb_out, inv_out,
    x_v, x_sem, x1, r1, c1, slab, lhs, ct, acc,
):
    def x_copy(ch):
        cols = pl.ds(pl.multiple_of(ch * CHUNK, CHUNK), CHUNK)
        return pltpu.make_async_copy(x_hbm.at[:, cols], x_v.at[:, cols], x_sem.at[ch])

    for ch in range(NCH):
        x_copy(ch).start()
    c = c_ref[...]
    gram_c = dot_hi(c.T, c)
    inv1 = inverse(gb_ref[...] * gram_c, x1, r1, c1)
    gram_a = dot_hi(dot_hi(inv1, g_ref[...]), inv1)
    down, across = diagonals(gram_a)
    down = 1.0 / jnp.sqrt(down / ROWS_A + EPS)
    across = 1.0 / jnp.sqrt(across / ROWS_A + EPS)
    a_out[...] = dot_hi(m16_ref[...], inv1) * across
    slab[...] = dot_hi(ms_ref[...].astype(F32), inv1) * across

    inv_out[...] = inverse(gram_a * down * across * gram_c, x1, r1, c1)

    count = cnt[0, 0]
    for s in range(SLOTS):
        p = pos[s, 0]
        tile = slab[pl.ds(pl.multiple_of(lax.shift_right_logical(p, 1) * BLK, BLK), BLK), :].T
        for jb in range(JBD):
            keep = jnp.where((count > s) & ((p & 1) == jb), 1.0, 0.0)
            lhs[jb * R:(jb + 1) * R, s * BLK:(s + 1) * BLK] = (tile * keep).astype(BF16)
    c_low = c.astype(BF16).astype(F32).T
    for jb in range(JBD):
        for t in range(CHUNK // K):
            ct[jb * R:(jb + 1) * R, t * K:(t + 1) * K] = c_low
    acc[...] = jnp.zeros_like(acc)

    def mode_two(ch, carry):
        x_copy(ch).wait()
        x = x_v[:, pl.ds(pl.multiple_of(ch * CHUNK, CHUNK), CHUNK)]
        t = jnp.dot(lhs[...], x, preferred_element_type=F32)
        t = (t * ct[...]).astype(BF16)
        j = lax.shift_right_logical(lax.broadcasted_iota(jnp.int32, (CHUNK, BLK), 0), 6) + ch * JPC
        ones = jnp.where(j == lax.broadcasted_iota(jnp.int32, (CHUNK, BLK), 1), 1.0, 0.0).astype(BF16)
        acc[...] += jnp.dot(t, ones, preferred_element_type=F32)
        return carry

    lax.fori_loop(0, NCH, mode_two, 0)
    for jb in range(JBD):
        pb_out[jb * BLK:(jb + 1) * BLK, :] = acc[jb * R:(jb + 1) * R, :].T.astype(BF16)


def kernel_c(pb_ref, inv_ref, b_out, pb_recv, sq_piece, sq_row, sq_all, sq_col, send, recv):
    me_r = lax.axis_index("row")
    barrier, partners = greet((("row", NROW), ("col", NCOL)))
    pl.semaphore_wait(barrier, partners)
    scatter("row", NROW, pb_ref, pb_recv, send.at[0], recv.at[0])
    wait_bytes(pb_recv, recv.at[0])
    m2 = pb_ref[me_r].astype(F32) + jnp.sum(pb_recv[...].astype(F32), axis=0)
    raw = dot_hi(m2, inv_ref[...])
    sq_piece[...] = jnp.sum(raw * raw, axis=0, keepdims=True)
    spread("row", NROW, sq_piece, sq_row, send.at[1], recv.at[1])
    wait_bytes(sq_row, recv.at[1])
    sq_all[...] = sq_piece[...] + jnp.sum(sq_row[...], axis=0)
    spread("col", NCOL, sq_all, sq_col, send.at[2], recv.at[2])
    wait_bytes(sq_col, recv.at[2])
    squares = sq_all[...] + jnp.sum(sq_col[...], axis=0)
    b_out[...] = raw / jnp.sqrt(squares / ROWS_B + EPS)
    wait_bytes(pb_recv, send.at[0])
    wait_bytes(sq_row, send.at[1])
    wait_bytes(sq_col, send.at[2])


VM = pl.BlockSpec(memory_space=pltpu.VMEM)
SM = pl.BlockSpec(memory_space=pltpu.SMEM)
ANY = pl.BlockSpec(memory_space=pl.ANY)


def shape(dims, kind=F32):
    return jax.ShapeDtypeStruct(dims, kind)


def body(blocks, factor_b, factor_c, block_pos, block_count):
    flat = blocks.reshape(SLOTS * BLK, WIDE)
    vm, dma = pltpu.VMEM, pltpu.SemaphoreType.DMA
    gram_b, m16, ms, g = pl.pallas_call(
        kernel_a,
        name="mode_one",
        out_shape=(shape((R, R)), shape((SHARE_A, R)), shape((SLAB_A, R), BF16), shape((R, R))),
        in_specs=[SM, SM, ANY, VM, VM],
        out_specs=[VM] * 4,
        scratch_shapes=[
            vm((SLAB_A, WIDE), BF16), dma((NCH,)), vm((R, R), F32), vm((CHUNK, JBD * R), BF16), vm((SLAB_A, JBD * R), F32),
            vm((R, R), F32), vm((NCOL, 1, R), F32), vm((NCOL - 1, 1, R), F32), vm((NCOL, 1, R), F32), vm((NROW, 32, R), F32),
            vm((NCOL, SHARE_A, R), BF16), vm((NCOL - 1, SHARE_A, R), BF16), vm((NCOL, SHARE_A, R), BF16),
            vm((NROW - 1, 8, R), F32), vm((8, R), F32), vm((NCOL, 8, R), F32),
            dma((7,)), dma((7,)),
        ],
        compiler_params=pltpu.CompilerParams(collective_id=0, has_side_effects=True),
    )(block_pos, block_count, flat, factor_b, factor_c)
    hat_a, part_b, inv = pl.pallas_call(
        kernel_b,
        name="solve_two",
        out_shape=(shape((SHARE_A, R)), shape((SLAB_B, R), BF16), shape((R, R))),
        in_specs=[SM, SM, ANY, VM, VM, VM, VM, VM],
        out_specs=[VM] * 3,
        scratch_shapes=[
            vm((SLAB_A, WIDE), BF16), dma((NCH,)), vm((R, R), F32), vm((R, R), F32), vm((R, R), F32),
            vm((SLAB_A, R), F32), vm((JBD * R, SLAB_A), BF16), vm((JBD * R, CHUNK), F32), vm((JBD * R, BLK), F32),
        ],
    )(block_pos, block_count, flat, factor_c, gram_b, m16, ms, g)
    hat_b = pl.pallas_call(
        kernel_c,
        name="mode_two",
        out_shape=shape((SHARE_B, R)),
        in_specs=[VM, VM],
        out_specs=VM,
        scratch_shapes=[
            vm((NROW - 1, SHARE_B, R), BF16), vm((1, R), F32), vm((NROW - 1, 1, R), F32), vm((1, R), F32),
            vm((NCOL - 1, 1, R), F32), dma((3,)), dma((3,)),
        ],
        compiler_params=pltpu.CompilerParams(collective_id=1, has_side_effects=True),
    )(part_b.reshape(NROW, SHARE_B, R), inv)
    return hat_a, hat_b


def solution(mesh):
    return jax.shard_map(
        body,
        mesh=mesh,
        in_specs=(P("row", "col", None), P("col", None), P(), P("row", "col"), P("row", "col")),
        out_specs=(P(("row", "col"), None), P(("col", "row"), None)),
        check_vma=False,
    )
```

time: 724 us -> 106 us (0.15); the launches traced: 712 us -> 105 us
  waiting for transfers between devices: 441 us -> 0 us
  other arithmetic: 110 us -> 0 us
  Pallas kernels: 0 us -> 101 us
  blocking collectives: 78.7 us -> 0 us
  local copies, waits for them, and re-layouts: 36.9 us -> 2.69 us
  matrix products: 19.6 us -> 0 us
  between operations: 17.1 us -> 1.3 us
  loops' own time: 8.05 us -> 0 us
    psum x2 -> x0, waiting for transfers between devices: 387 us -> none  [the longest x1 314 us: body(): sum_a = lax.psum(partial_a, 'col')]
    another operation x18 -> x0, other arithmetic: 108 us -> none  [the longest x13 68.6 us: solve_right(): lower = jnp.linalg.cholesky(matrix)]
    pallas_call x0 -> x3, Pallas kernels: none -> 101 us  [the longest x1 52.1 us: body(): pl.pallas_call(kernel_a, name='mode_one', out_shape=(shape((R, R)), shape...]
    psum x1 -> x0, blocking collectives: 78.7 us -> none  [body(): squares_b = lax.psum(jnp.sum(new_b * new_b, axis=0), ('row', 'col'))]
    reduce_scatter x1 -> x0, waiting for transfers between devices: 54.3 us -> none  [body(): part_b = lax.psum_scatter(partial_b, 'row', scatter_dimension=0, tiled=True)]
    dot_general x5 -> x0, matrix products: 13.7 us -> none  [the longest x1 4.64 us: second_term(): lax.dot_general(cube, c_low, (((2,), (0,)), ((), ())), preferred_element_...]
    while x1 -> x0, local copies, waits for them, and re-layouts: 12 us -> none  [body(): lax.fori_loop(0, live_count, mode_one, jnp.zeros((row_slab, rank_width),...]
    another operation x4 -> x0, loops' own time: 8.05 us -> none  [the longest x1 4.1 us: body(): lax.fori_loop(0, live_count, mode_two, jnp.zeros((col_slab, rank_width),...]
  transfers between devices with their start and end apart: 3 -> 0, of which waited for: 3 -> 0; matrix products, arithmetic and copies ran while one was open for 3% -> 0% of each run, Pallas kernels for 0% -> 0%
where the time goes in v1:
time: 106 us; the launch traced here: 105 us
  Pallas kernels  101 us (95%)
  local copies, waits for them, and re-layouts  2.69 us (3%)
  between operations  1.3 us (1%)
    pallas_call x1, Pallas kernels, body(): pl.pallas_call(kernel_a, name='mode_one', out_shape=(shape((R, R)), shape...  52.1 us
    pallas_call x1, Pallas kernels, body(): pl.pallas_call(kernel_b, name='solve_two', out_shape=(shape((SHARE_A, R))...  28.1 us
    pallas_call x1, Pallas kernels, body(): pl.pallas_call(kernel_c, name='mode_two', out_shape=shape((SHARE_B, R)),...  21.2 us
    unnamed x2, local copies, waits for them, and re-layouts  2.69 us

profile of v1, /device:TPU:1, one launch (start us, length us, event | category | flops | bytes accessed | tf_op | source)
XLA Modules:
  0.0 105.4 jit_solution(17691164722767024135)
XLA Ops:
  1.3 1.3 %copy.8.pos = s32[4,1]{1,0:T(4,128)} copy(s32[4,1]{0,1:T(1,128)} %param.8) | data formatting | bytes 32 | tf_op args[3]
  2.6 52.1 %mode_one.1 = (f32[256,256]{1,0:T(8,128)}, f32[16,256]{1,0:T(8,128)}, bf16[512,256]{1,0:T(8,128)(2,1)}, f32[256,256]{1,0:T(8,128)}) custom-call(s32[4,1]{1,0:T(4,128)} %copy.8.pos, s32[1,1]{1,0:T(1,128)S(6)} %copy.10.cnt, bf16[512,8192]{1,0:T(8,128)(2,1)} %bitcast.2, f32[256,256]{1,0:T(8,128)} %b_ref.1, f32[64,256]{1,0:T(8,128)} %c_ref.3), custom_call_target="tpu_custom_call" | custom-call | tf_op jit(solution)/shard_map/mode_one/pallas_call | solution.py:315
  54.7 28.1 %solve_two.1 = (f32[16,256]{1,0:T(8,128)}, bf16[256,256]{1,0:T(8,128)(2,1)}, f32[256,256]{1,0:T(8,128)}) custom-call(s32[4,1]{1,0:T(4,128)} %copy.8.pos, s32[1,1]{1,0:T(1,128)S(6)} %copy.10.cnt, bf16[512,8192]{1,0:T(8,128)(2,1)} %bitcast.3, f32[64,256]{1,0:T(8,128)} %c_ref.3, f32[256,256]{1,0:T(8,128)} %get-tuple-element.9.gb_ref, ...), custom_call_target="tpu_custom_call" | custom-call | tf_op jit(solution)/shard_map/solve_two/pallas_call | solution.py:330
  82.8 21.2 %mode_two.1 = f32[32,256]{1,0:T(8,128)} custom-call(bf16[8,32,256]{2,1,0:T(8,128)(2,1)} %bitcast.4, f32[256,256]{1,0:T(8,128)} %get-tuple-element.15.inv_ref), custom_call_target="tpu_custom_call" | custom-call | tf_op jit(solution)/shard_map/mode_two/pallas_call | solution.py:341
  104.0 1.4 %copy.11 = f32[32,256]{1,0:T(8,128)} copy(f32[32,256]{1,0:T(8,128)} %mode_two.1) | data formatting | bytes 65536

commit v2 on v1

--- a/solution.py
+++ b/solution.py
@@ -21,6 +21,8 @@
 JPC = CHUNK // K
 SHARE_A = SLAB_A // NCOL
 SHARE_B = SLAB_B // NROW
+CHIPS = NCOL // 2
+SHARE_G = BLK // NROW
 ROWS_A = SLAB_A * NROW
 ROWS_B = SLAB_B * NCOL
 EPS = 1e-06
@@ -97,10 +99,18 @@
     gb_out, m16_out, ms_out, g_out,
     x_v, x_sem, br, w_v, acc,
     gram, gb_part, gb_recv, gb_col, gb_full,
-    part, m_recv, ms, g_recv, g_piece, g_full,
+    part, pair_recv, half, m_recv, ms, g_piece, g_recv, g_full,
     send, recv,
 ):
     me_r, me_c = lax.axis_index("row"), lax.axis_index("col")
+    chip, core = me_c // 2, lax.rem(me_c, 2)
+    mate = chip * 2 + 1 - core
+
+    def to_mate(src, dst, n):
+        pltpu.make_async_remote_copy(
+            src_ref=src, dst_ref=dst, send_sem=send.at[n], recv_sem=recv.at[n],
+            device_id={"col": mate}, device_id_type=MESH,
+        ).start()
 
     def x_copy(ch):
         cols = pl.ds(pl.multiple_of(ch * CHUNK, CHUNK), CHUNK)
@@ -129,62 +139,92 @@
         acc[...] += jnp.dot(x, w_v[...], preferred_element_type=F32)
         return carry
 
-    lax.fori_loop(0, NCH, mode_one, 0)
+    lax.fori_loop(0, NCH - 3, mode_one, 0)
+    pl.semaphore_wait(barrier, partners)
+    scatter("col", NCOL, gb_part, gb_recv, send.at[0], recv.at[0])
+    lax.fori_loop(NCH - 3, NCH, mode_one, 0)
+
     count = cnt[0, 0]
     for ib in range(IBD):
         total = jnp.zeros((BLK, R), F32)
         for s in range(SLOTS):
-            p = pos[s, 0]
+            p = pos[0, s]
             live = jnp.where(count > s, 1.0, 0.0).astype(F32)
             for jb in range(JBD):
                 keep = jnp.where(p == ib * JBD + jb, live, 0.0)
                 total += acc[s * BLK:(s + 1) * BLK, jb * R:(jb + 1) * R] * keep
-        low = total.astype(BF16)
         for t in range(BLK // SHARE_A):
-            part[ib * (BLK // SHARE_A) + t] = low[t * SHARE_A:(t + 1) * SHARE_A, :]
-
-    pl.semaphore_wait(barrier, partners)
-    scatter("col", NCOL, gb_part, gb_recv, send.at[0], recv.at[0])
-    scatter("col", NCOL, part, m_recv, send.at[1], recv.at[1])
+            at = ib * (BLK // SHARE_A) + t
+            part[at % 2, at // 2] = total[t * SHARE_A:(t + 1) * SHARE_A, :]
+
+    to_mate(part.at[1 - core], pair_recv, 1)
+    wait_bytes(pair_recv, recv.at[1])
+    half[...] = (part[core] + pair_recv[...]).astype(BF16)
+
+    def to_chip(k, carry):
+        d = lax.rem(chip + k, CHIPS)
+        pltpu.make_async_remote_copy(
+            src_ref=half.at[d], dst_ref=m_recv.at[k - 1], send_sem=send.at[2], recv_sem=recv.at[2],
+            device_id={"col": d * 2 + core}, device_id_type=MESH,
+        ).start()
+        return carry
+
+    lax.fori_loop(1, CHIPS, to_chip, 0)
 
     wait_bytes(gb_recv, recv.at[0])
     gb_col[me_c] = gb_part[me_c] + jnp.sum(gb_recv[...], axis=0)
-    gather("col", NCOL, gb_col.at[me_c], send.at[2], recv.at[2])
-
-    wait_bytes(m_recv, recv.at[1])
-    m16 = part[me_c].astype(F32) + jnp.sum(m_recv[...].astype(F32), axis=0)
+    gather("col", NCOL, gb_col.at[me_c], send.at[3], recv.at[3])
+
+    wait_bytes(m_recv, recv.at[2])
+    m16 = part[core, chip] + pair_recv[chip] + jnp.sum(m_recv[...].astype(F32), axis=0)
+    ms[core, chip] = m16.astype(BF16)
+
+    def from_chip(k, carry):
+        piece = ms.at[core, chip]
+        pltpu.make_async_remote_copy(
+            src_ref=piece, dst_ref=piece, send_sem=send.at[4], recv_sem=recv.at[4],
+            device_id={"col": lax.rem(chip + k, CHIPS) * 2 + core}, device_id_type=MESH,
+        ).start()
+        return carry
+
+    lax.fori_loop(1, CHIPS, from_chip, 0)
     m16_out[...] = m16
-    ms[me_c] = m16.astype(BF16)
-    gather("col", NCOL, ms.at[me_c], send.at[3], recv.at[3])
-
-    wait_bytes(gb_col.at[pl.ds(0, NCOL - 1)], recv.at[2])
+
+    wait_bytes(gb_col.at[pl.ds(0, NCOL - 1)], recv.at[3])
     for i in range(32):
         gb_full[me_r, i:i + 1, :] = gb_col[i]
-    gather("row", NROW, gb_full.at[me_r], send.at[4], recv.at[4])
-
-    wait_bytes(ms.at[pl.ds(0, NCOL - 1)], recv.at[3])
+    gather("row", NROW, gb_full.at[me_r], send.at[5], recv.at[5])
+
+    wait_bytes(m_recv, recv.at[4])
+    to_mate(ms.at[core], ms.at[core], 6)
+    wait_bytes(ms.at[0], recv.at[6])
+
     slab = ms[...].reshape(SLAB_A, R)
-    ms_out[...] = slab
     gram[...] = jnp.dot(slab.T, slab, preferred_element_type=F32)
-    g_piece[...] = gram[pl.ds(pl.multiple_of(me_c * 8, 8), 8), :]
-    spread("row", NROW, g_piece, g_recv, send.at[5], recv.at[5])
-
-    wait_bytes(gb_full.at[pl.ds(0, NROW - 1)], recv.at[4])
+    g_piece[...] = gram[pl.ds(pl.multiple_of(core * BLK, BLK), BLK), :].reshape(NROW, SHARE_G, R)
+    scatter("row", NROW, g_piece, g_recv, send.at[7], recv.at[7])
+    for at in range(NCOL):
+        ms_out[at * SHARE_A:(at + 1) * SHARE_A, :] = ms[at % 2, at // 2]
+    wait_bytes(g_recv, recv.at[7])
+    g_full[core, me_r] = g_piece[me_r] + jnp.sum(g_recv[...], axis=0)
+    gather("row", NROW, g_full.at[core, me_r], send.at[8], recv.at[8])
+    wait_bytes(gb_full.at[pl.ds(0, NROW - 1)], recv.at[5])
     gb_out[...] = gb_full[...].reshape(R, R)
-
-    wait_bytes(g_recv, recv.at[5])
-    g_full[me_c] = g_piece[...] + jnp.sum(g_recv[...], axis=0)
-    gather("col", NCOL, g_full.at[me_c], send.at[6], recv.at[6])
-    wait_bytes(g_full.at[pl.ds(0, NCOL - 1)], recv.at[6])
+    wait_bytes(g_recv, recv.at[8])
+    to_mate(g_full.at[core], g_full.at[core], 9)
+    wait_bytes(g_full.at[0], recv.at[9])
     g_out[...] = g_full[...].reshape(R, R)
 
     wait_bytes(gb_recv, send.at[0])
-    wait_bytes(m_recv, send.at[1])
-    wait_bytes(gb_col.at[pl.ds(0, NCOL - 1)], send.at[2])
-    wait_bytes(ms.at[pl.ds(0, NCOL - 1)], send.at[3])
-    wait_bytes(gb_full.at[pl.ds(0, NROW - 1)], send.at[4])
-    wait_bytes(g_recv, send.at[5])
-    wait_bytes(g_full.at[pl.ds(0, NCOL - 1)], send.at[6])
+    wait_bytes(pair_recv, send.at[1])
+    wait_bytes(m_recv, send.at[2])
+    wait_bytes(gb_col.at[pl.ds(0, NCOL - 1)], send.at[3])
+    wait_bytes(m_recv, send.at[4])
+    wait_bytes(gb_full.at[pl.ds(0, NROW - 1)], send.at[5])
+    wait_bytes(ms.at[0], send.at[6])
+    wait_bytes(g_recv, send.at[7])
+    wait_bytes(g_recv, send.at[8])
+    wait_bytes(g_full.at[0], send.at[9])
 
 
 def eye():
@@ -229,16 +269,10 @@
 
 
 def kernel_b(
-    pos, cnt, x_hbm, c_ref, gb_ref, m16_ref, ms_ref, g_ref,
-    a_out, pb_out, inv_out,
-    x_v, x_sem, x1, r1, c1, slab, lhs, ct, acc,
+    pos, cnt, c_ref, gb_ref, m16_ref, ms_ref, g_ref,
+    a_out, lhs_out, inv_out,
+    x1, r1, c1, slab,
 ):
-    def x_copy(ch):
-        cols = pl.ds(pl.multiple_of(ch * CHUNK, CHUNK), CHUNK)
-        return pltpu.make_async_copy(x_hbm.at[:, cols], x_v.at[:, cols], x_sem.at[ch])
-
-    for ch in range(NCH):
-        x_copy(ch).start()
     c = c_ref[...]
     gram_c = dot_hi(c.T, c)
     inv1 = inverse(gb_ref[...] * gram_c, x1, r1, c1)
@@ -253,12 +287,28 @@
 
     count = cnt[0, 0]
     for s in range(SLOTS):
-        p = pos[s, 0]
+        p = pos[0, s]
         tile = slab[pl.ds(pl.multiple_of(lax.shift_right_logical(p, 1) * BLK, BLK), BLK), :].T
         for jb in range(JBD):
             keep = jnp.where((count > s) & ((p & 1) == jb), 1.0, 0.0)
-            lhs[jb * R:(jb + 1) * R, s * BLK:(s + 1) * BLK] = (tile * keep).astype(BF16)
-    c_low = c.astype(BF16).astype(F32).T
+            lhs_out[jb * R:(jb + 1) * R, s * BLK:(s + 1) * BLK] = (tile * keep).astype(BF16)
+
+
+def kernel_c(
+    x_hbm, c_ref, lhs, inv_ref,
+    b_out,
+    x_v, x_sem, ct, acc, pb, pb_recv, sq_piece, sq_row, sq_all, sq_col, send, recv,
+):
+    me_r = lax.axis_index("row")
+
+    def x_copy(ch):
+        cols = pl.ds(pl.multiple_of(ch * CHUNK, CHUNK), CHUNK)
+        return pltpu.make_async_copy(x_hbm.at[:, cols], x_v.at[:, cols], x_sem.at[ch])
+
+    for ch in range(NCH):
+        x_copy(ch).start()
+    barrier, partners = greet((("row", NROW), ("col", NCOL)))
+    c_low = c_ref[...].astype(BF16).astype(F32).T
     for jb in range(JBD):
         for t in range(CHUNK // K):
             ct[jb * R:(jb + 1) * R, t * K:(t + 1) * K] = c_low
@@ -276,16 +326,14 @@
 
     lax.fori_loop(0, NCH, mode_two, 0)
     for jb in range(JBD):
-        pb_out[jb * BLK:(jb + 1) * BLK, :] = acc[jb * R:(jb + 1) * R, :].T.astype(BF16)
-
-
-def kernel_c(pb_ref, inv_ref, b_out, pb_recv, sq_piece, sq_row, sq_all, sq_col, send, recv):
-    me_r = lax.axis_index("row")
-    barrier, partners = greet((("row", NROW), ("col", NCOL)))
+        rows = acc[jb * R:(jb + 1) * R, :].T.astype(BF16)
+        for t in range(BLK // SHARE_B):
+            pb[jb * (BLK // SHARE_B) + t] = rows[t * SHARE_B:(t + 1) * SHARE_B, :]
+
     pl.semaphore_wait(barrier, partners)
-    scatter("row", NROW, pb_ref, pb_recv, send.at[0], recv.at[0])
+    scatter("row", NROW, pb, pb_recv, send.at[0], recv.at[0])
     wait_bytes(pb_recv, recv.at[0])
-    m2 = pb_ref[me_r].astype(F32) + jnp.sum(pb_recv[...].astype(F32), axis=0)
+    m2 = pb[me_r].astype(F32) + jnp.sum(pb_recv[...].astype(F32), axis=0)
     raw = dot_hi(m2, inv_ref[...])
     sq_piece[...] = jnp.sum(raw * raw, axis=0, keepdims=True)
     spread("row", NROW, sq_piece, sq_row, send.at[1], recv.at[1])
@@ -311,6 +359,7 @@
 
 def body(blocks, factor_b, factor_c, block_pos, block_count):
     flat = blocks.reshape(SLOTS * BLK, WIDE)
+    place = block_pos.T
     vm, dma = pltpu.VMEM, pltpu.SemaphoreType.DMA
     gram_b, m16, ms, g = pl.pallas_call(
         kernel_a,
@@ -321,35 +370,35 @@
         scratch_shapes=[
             vm((SLAB_A, WIDE), BF16), dma((NCH,)), vm((R, R), F32), vm((CHUNK, JBD * R), BF16), vm((SLAB_A, JBD * R), F32),
             vm((R, R), F32), vm((NCOL, 1, R), F32), vm((NCOL - 1, 1, R), F32), vm((NCOL, 1, R), F32), vm((NROW, 32, R), F32),
-            vm((NCOL, SHARE_A, R), BF16), vm((NCOL - 1, SHARE_A, R), BF16), vm((NCOL, SHARE_A, R), BF16),
-            vm((NROW - 1, 8, R), F32), vm((8, R), F32), vm((NCOL, 8, R), F32),
-            dma((7,)), dma((7,)),
+            vm((2, CHIPS, SHARE_A, R), F32), vm((CHIPS, SHARE_A, R), F32), vm((CHIPS, SHARE_A, R), BF16),
+            vm((CHIPS - 1, SHARE_A, R), BF16), vm((2, CHIPS, SHARE_A, R), BF16),
+            vm((NROW, SHARE_G, R), F32), vm((NROW - 1, SHARE_G, R), F32), vm((2, NROW, SHARE_G, R), F32),
+            dma((10,)), dma((10,)),
         ],
         compiler_params=pltpu.CompilerParams(collective_id=0, has_side_effects=True),
-    )(block_pos, block_count, flat, factor_b, factor_c)
-    hat_a, part_b, inv = pl.pallas_call(
+    )(place, block_count, flat, factor_b, factor_c)
+    hat_a, lhs, inv = pl.pallas_call(
         kernel_b,
         name="solve_two",
-        out_shape=(shape((SHARE_A, R)), shape((SLAB_B, R), BF16), shape((R, R))),
-        in_specs=[SM, SM, ANY, VM, VM, VM, VM, VM],
+        out_shape=(shape((SHARE_A, R)), shape((JBD * R, SLAB_A), BF16), shape((R, R))),
+        in_specs=[SM, SM, VM, VM, VM, VM, VM],
         out_specs=[VM] * 3,
-        scratch_shapes=[
-            vm((SLAB_A, WIDE), BF16), dma((NCH,)), vm((R, R), F32), vm((R, R), F32), vm((R, R), F32),
-            vm((SLAB_A, R), F32), vm((JBD * R, SLAB_A), BF16), vm((JBD * R, CHUNK), F32), vm((JBD * R, BLK), F32),
-        ],
-    )(block_pos, block_count, flat, factor_c, gram_b, m16, ms, g)
+        scratch_shapes=[vm((R, R), F32), vm((R, R), F32), vm((R, R), F32), vm((SLAB_A, R), F32)],
+    )(place, block_count, factor_c, gram_b, m16, ms, g)
     hat_b = pl.pallas_call(
         kernel_c,
         name="mode_two",
         out_shape=shape((SHARE_B, R)),
-        in_specs=[VM, VM],
+        in_specs=[ANY, VM, VM, VM],
         out_specs=VM,
         scratch_shapes=[
-            vm((NROW - 1, SHARE_B, R), BF16), vm((1, R), F32), vm((NROW - 1, 1, R), F32), vm((1, R), F32),
-            vm((NCOL - 1, 1, R), F32), dma((3,)), dma((3,)),
+            vm((SLAB_A, WIDE), BF16), dma((NCH,)), vm((JBD * R, CHUNK), F32), vm((JBD * R, BLK), F32),
+            vm((NROW, SHARE_B, R), BF16), vm((NROW - 1, SHARE_B, R), BF16),
+            vm((1, R), F32), vm((NROW - 1, 1, R), F32), vm((1, R), F32), vm((NCOL - 1, 1, R), F32),
+            dma((3,)), dma((3,)),
         ],
         compiler_params=pltpu.CompilerParams(collective_id=1, has_side_effects=True),
-    )(part_b.reshape(NROW, SHARE_B, R), inv)
+    )(flat, factor_c, lhs, inv)
     return hat_a, hat_b
 
 

time: 106 us -> 93.8 us (0.88)
  Pallas kernels: 101 us -> 90.9 us
  local copies, waits for them, and re-layouts: 2.69 us -> 1.38 us
    pallas_call x1, Pallas kernels: 52.1 us -> 43.2 us  [body(): pl.pallas_call(kernel_a, name='mode_one', out_shape=(shape((R, R)), shape...]
    pallas_call x1, Pallas kernels: 28.1 us -> 19.8 us  [body(): pl.pallas_call(kernel_b, name='solve_two', out_shape=(shape((SHARE_A, R))...]
    pallas_call x1, Pallas kernels: 21.2 us -> 27.9 us  [body(): pl.pallas_call(kernel_c, name='mode_two', out_shape=shape((SHARE_B, R)),...]
    unnamed x2 -> x1, local copies, waits for them, and re-layouts: 2.69 us -> 1.38 us
where the time goes in v2:
time: 93.8 us; the launch traced here: 93.6 us
  Pallas kernels  90.9 us (97%)
  local copies, waits for them, and re-layouts  1.38 us (1%)
  between operations  1.29 us (1%)
    pallas_call x1, Pallas kernels, body(): pl.pallas_call(kernel_a, name='mode_one', out_shape=(shape((R, R)), shape...  43.2 us
    pallas_call x1, Pallas kernels, body(): pl.pallas_call(kernel_c, name='mode_two', out_shape=shape((SHARE_B, R)),...  27.9 us
    pallas_call x1, Pallas kernels, body(): pl.pallas_call(kernel_b, name='solve_two', out_shape=(shape((SHARE_A, R))...  19.8 us

profile of v2, /device:TPU:1, one launch (start us, length us, event | category | flops | bytes accessed | tf_op | source)
XLA Modules:
  0.0 93.6 jit_solution(15686102534928793253)
XLA Ops:
  1.3 43.2 %mode_one.1 = (f32[256,256]{1,0:T(8,128)}, f32[16,256]{1,0:T(8,128)}, bf16[512,256]{1,0:T(8,128)(2,1)}, f32[256,256]{1,0:T(8,128)}) custom-call(s32[1,4]{1,0:T(1,128)} %bitcast.4, s32[1,1]{1,0:T(1,128)S(6)} %copy.8.cnt, bf16[512,8192]{1,0:T(8,128)(2,1)} %bitcast.2, f32[256,256]{1,0:T(8,128)} %b_ref.1, f32[64,256]{1,0:T(8,128)} %c_ref.5), custom_call_target="tpu_custom_call" | custom-call | tf_op jit(solution)/shard_map/mode_one/pallas_call | solution.py:364
  44.5 19.8 %solve_two.1 = (f32[16,256]{1,0:T(8,128)}, bf16[512,512]{1,0:T(8,128)(2,1)}, f32[256,256]{1,0:T(8,128)}) custom-call(s32[1,4]{1,0:T(1,128)} %bitcast.5, s32[1,1]{1,0:T(1,128)S(6)} %copy.8.cnt, f32[64,256]{1,0:T(8,128)} %c_ref.5, f32[256,256]{1,0:T(8,128)} %get-tuple-element.9.gb_ref, f32[16,256]{1,0:T(8,128)} %get-tuple-element.10.m16_ref, ...), custom_call_target="tpu_custom_call" | custom-call | tf_op jit(solution)/shard_map/solve_two/pallas_call | solution.py:380
  64.3 27.9 %mode_two.1 = f32[32,256]{1,0:T(8,128)} custom-call(bf16[512,8192]{1,0:T(8,128)(2,1)} %bitcast.3, f32[64,256]{1,0:T(8,128)} %c_ref.5, bf16[512,512]{1,0:T(8,128)(2,1)} %get-tuple-element.14.lhs, f32[256,256]{1,0:T(8,128)} %get-tuple-element.15.inv_ref), custom_call_target="tpu_custom_call" | custom-call | tf_op jit(solution)/shard_map/mode_two/pallas_call | solution.py:388
  92.2 1.4 %copy.9 = f32[32,256]{1,0:T(8,128)} copy(f32[32,256]{1,0:T(8,128)} %mode_two.1) | data formatting | bytes 65536

commit v3 on v2

--- a/solution.py
+++ b/solution.py
@@ -348,6 +348,223 @@
     wait_bytes(sq_col, send.at[2])
 
 
+def low_dot(a, b):
+    return jnp.dot(a.astype(BF16), b.astype(BF16), preferred_element_type=F32)
+
+
+def short_inverse(v):
+    down, across = diagonals(v)
+    down, across = 1.0 / jnp.sqrt(down), 1.0 / jnp.sqrt(across)
+    unit = jnp.where(eye(), 1.0, 0.0)
+    c = v * down * across
+    norm = jnp.max(jnp.sum(jnp.abs(c), axis=0, keepdims=True), axis=1, keepdims=True)
+    alpha = jnp.where(norm < 1.9, 1.0, 1.0 / norm)
+    res = unit - alpha * c
+    x = alpha * (unit + res)
+    x = x + low_dot(x, low_dot(res, res))
+    x = x + low_dot(x, unit - dot_hi(c, x))
+    res = unit - dot_hi(c, x)
+    worst = jnp.max(jnp.sum(jnp.abs(res), axis=0, keepdims=True), axis=1, keepdims=True)
+    x = x + low_dot(x, res)
+    return x * down * across, worst
+
+
+def kernel_m(
+    pos, cnt, x_hbm, b_ref, c_ref,
+    a_out, b_out, worst_out,
+    x_v, x_sem, br, w_v, acc,
+    gram, gb_part, gb_recv, gb_col, gb_full,
+    part, pair_recv, half, m_recv, ms, m16, g_piece, g_recv, g_full,
+    gram_c, inv1, slab, turned, lhs, ct, acc2,
+    pb, pb_recv, sq_piece, sq_row, sq_all, sq_col,
+    send, recv,
+):
+    me_r, me_c = lax.axis_index("row"), lax.axis_index("col")
+    chip, core = me_c // 2, lax.rem(me_c, 2)
+    mate = chip * 2 + 1 - core
+
+    def to_mate(src, dst, n):
+        pltpu.make_async_remote_copy(
+            src_ref=src, dst_ref=dst, send_sem=send.at[n], recv_sem=recv.at[n],
+            device_id={"col": mate}, device_id_type=MESH,
+        ).start()
+
+    def chunk(ch):
+        return pl.ds(pl.multiple_of(ch * CHUNK, CHUNK), CHUNK)
+
+    def x_copy(ch):
+        return pltpu.make_async_copy(x_hbm.at[:, chunk(ch)], x_v.at[:, chunk(ch)], x_sem.at[ch])
+
+    for ch in range(NCH):
+        x_copy(ch).start()
+    barrier, partners = greet((("col", NCOL), ("row", NROW)))
+
+    b = b_ref[...]
+    gram[...] = dot_hi(b.T, b)
+    rows = gram[pl.ds(pl.multiple_of(me_r * 32, 32), 32), :]
+    for i in range(32):
+        gb_part[i] = rows[i:i + 1, :]
+    br[...] = b.astype(BF16).astype(F32)
+    cr = c_ref[...].astype(BF16).astype(F32)
+    acc[...] = jnp.zeros_like(acc)
+
+    def mode_one(ch, carry):
+        for jb in range(JBD):
+            tile = br[pl.ds(pl.multiple_of(jb * BLK + ch * JPC, JPC), JPC), :]
+            for j in range(JPC):
+                w_v[j * K:(j + 1) * K, jb * R:(jb + 1) * R] = (tile[j:j + 1, :] * cr).astype(BF16)
+        x_copy(ch).wait()
+        acc[...] += jnp.dot(x_v[:, chunk(ch)], w_v[...], preferred_element_type=F32)
+        return carry
+
+    lax.fori_loop(0, NCH - 3, mode_one, 0)
+    pl.semaphore_wait(barrier, partners)
+    scatter("col", NCOL, gb_part, gb_recv, send.at[0], recv.at[0])
+    lax.fori_loop(NCH - 3, NCH, mode_one, 0)
+
+    count = cnt[0, 0]
+    for ib in range(IBD):
+        total = jnp.zeros((BLK, R), F32)
+        for s in range(SLOTS):
+            p = pos[0, s]
+            live = jnp.where(count > s, 1.0, 0.0).astype(F32)
+            for jb in range(JBD):
+                keep = jnp.where(p == ib * JBD + jb, live, 0.0)
+                total += acc[s * BLK:(s + 1) * BLK, jb * R:(jb + 1) * R] * keep
+        for t in range(BLK // SHARE_A):
+            at = ib * (BLK // SHARE_A) + t
+            part[at % 2, at // 2] = total[t * SHARE_A:(t + 1) * SHARE_A, :]
+
+    to_mate(part.at[1 - core], pair_recv, 1)
+    c = c_ref[...]
+    gram_c[...] = dot_hi(c.T, c)
+    wait_bytes(pair_recv, recv.at[1])
+    half[...] = (part[core] + pair_recv[...]).astype(BF16)
+
+    def to_chip(k, carry):
+        d = lax.rem(chip + k, CHIPS)
+        pltpu.make_async_remote_copy(
+            src_ref=half.at[d], dst_ref=m_recv.at[k - 1], send_sem=send.at[2], recv_sem=recv.at[2],
+            device_id={"col": d * 2 + core}, device_id_type=MESH,
+        ).start()
+        return carry
+
+    lax.fori_loop(1, CHIPS, to_chip, 0)
+
+    wait_bytes(gb_recv, recv.at[0])
+    gb_col[me_c] = gb_part[me_c] + jnp.sum(gb_recv[...], axis=0)
+    gather("col", NCOL, gb_col.at[me_c], send.at[3], recv.at[3])
+    c_low = cr.T
+    for jb in range(JBD):
+        for t in range(CHUNK // K):
+            ct[jb * R:(jb + 1) * R, t * K:(t + 1) * K] = c_low
+    acc2[...] = jnp.zeros_like(acc2)
+    wait_bytes(gb_col.at[pl.ds(0, NCOL - 1)], recv.at[3])
+    for i in range(32):
+        gb_full[me_r, i:i + 1, :] = gb_col[i]
+    gather("row", NROW, gb_full.at[me_r], send.at[5], recv.at[5])
+
+    wait_bytes(m_recv, recv.at[2])
+    mine = part[core, chip] + pair_recv[chip] + jnp.sum(m_recv[...].astype(F32), axis=0)
+    ms[core, chip] = mine.astype(BF16)
+
+    def from_chip(k, carry):
+        piece = ms.at[core, chip]
+        pltpu.make_async_remote_copy(
+            src_ref=piece, dst_ref=piece, send_sem=send.at[4], recv_sem=recv.at[4],
+            device_id={"col": lax.rem(chip + k, CHIPS) * 2 + core}, device_id_type=MESH,
+        ).start()
+        return carry
+
+    lax.fori_loop(1, CHIPS, from_chip, 0)
+
+    wait_bytes(gb_full.at[pl.ds(0, NROW - 1)], recv.at[5])
+    solved, worst_one = short_inverse(gb_full[...].reshape(R, R) * gram_c[...])
+    inv1[...] = solved
+    m16[...] = dot_hi(mine, solved)
+
+    wait_bytes(m_recv, recv.at[4])
+    to_mate(ms.at[core], ms.at[core], 6)
+    wait_bytes(ms.at[0], recv.at[6])
+    for at in range(NCOL):
+        slab[at * SHARE_A:(at + 1) * SHARE_A, :] = ms[at % 2, at // 2]
+
+    gram[...] = jnp.dot(slab[...].T, slab[...], preferred_element_type=F32)
+    g_piece[...] = gram[pl.ds(pl.multiple_of(core * BLK, BLK), BLK), :].reshape(NROW, SHARE_G, R)
+    scatter("row", NROW, g_piece, g_recv, send.at[7], recv.at[7])
+
+    top = inv1[...].astype(BF16)
+    rest = (inv1[...] - top.astype(F32)).astype(BF16)
+    last = (((1,), (1,)), ((), ()))
+    turned[...] = lax.dot_general(top, slab[...], last, preferred_element_type=F32) + lax.dot_general(
+        rest, slab[...], last, preferred_element_type=F32
+    )
+    for s in range(SLOTS):
+        p = pos[0, s]
+        live = jnp.where(count > s, 1.0, 0.0).astype(F32)
+        for jb in range(JBD):
+            tile = jnp.zeros((R, BLK), F32)
+            for ib in range(IBD):
+                tile += turned[:, ib * BLK:(ib + 1) * BLK] * jnp.where(p == ib * JBD + jb, live, 0.0)
+            lhs[jb * R:(jb + 1) * R, s * BLK:(s + 1) * BLK] = tile.astype(BF16)
+
+    def mode_two(ch, carry):
+        t = jnp.dot(lhs[...], x_v[:, chunk(ch)], preferred_element_type=F32)
+        t = (t * ct[...]).astype(BF16)
+        j = lax.shift_right_logical(lax.broadcasted_iota(jnp.int32, (CHUNK, BLK), 0), 6) + ch * JPC
+        ones = jnp.where(j == lax.broadcasted_iota(jnp.int32, (CHUNK, BLK), 1), 1.0, 0.0).astype(BF16)
+        acc2[...] += jnp.dot(t, ones, preferred_element_type=F32)
+        return carry
+
+    lax.fori_loop(0, NCH - 4, mode_two, 0)
+    wait_bytes(g_recv, recv.at[7])
+    g_full[core, me_r] = g_piece[me_r] + jnp.sum(g_recv[...], axis=0)
+    gather("row", NROW, g_full.at[core, me_r], send.at[8], recv.at[8])
+    lax.fori_loop(NCH - 4, NCH, mode_two, 0)
+    for jb in range(JBD):
+        rows = acc2[jb * R:(jb + 1) * R, :].T.astype(BF16)
+        for t in range(BLK // SHARE_B):
+            pb[jb * (BLK // SHARE_B) + t] = rows[t * SHARE_B:(t + 1) * SHARE_B, :]
+    wait_bytes(g_recv, recv.at[8])
+    to_mate(g_full.at[core], g_full.at[core], 9)
+    scatter("row", NROW, pb, pb_recv, send.at[10], recv.at[10])
+
+    wait_bytes(g_full.at[0], recv.at[9])
+    solved = inv1[...]
+    gram_a = dot_hi(dot_hi(solved, g_full[...].reshape(R, R)), solved)
+    down, across = diagonals(gram_a)
+    down = 1.0 / jnp.sqrt(down / ROWS_A + EPS)
+    across = 1.0 / jnp.sqrt(across / ROWS_A + EPS)
+    a_out[...] = m16[...] * across
+    inv2, worst_two = short_inverse(gram_a * down * across * gram_c[...])
+    worst_out[...] = jnp.full((8, 128), 1.0, F32) * jnp.maximum(worst_one, worst_two)
+
+    wait_bytes(pb_recv, recv.at[10])
+    m2 = (pb[me_r].astype(F32) + jnp.sum(pb_recv[...].astype(F32), axis=0)) * across
+    raw = dot_hi(m2, inv2)
+    sq_piece[...] = jnp.sum(raw * raw, axis=0, keepdims=True)
+    spread("row", NROW, sq_piece, sq_row, send.at[11], recv.at[11])
+    wait_bytes(sq_row, recv.at[11])
+    sq_all[...] = sq_piece[...] + jnp.sum(sq_row[...], axis=0)
+    spread("col", NCOL, sq_all, sq_col, send.at[12], recv.at[12])
+    wait_bytes(gb_recv, send.at[0])
+    wait_bytes(pair_recv, send.at[1])
+    wait_bytes(m_recv, send.at[2])
+    wait_bytes(gb_col.at[pl.ds(0, NCOL - 1)], send.at[3])
+    wait_bytes(m_recv, send.at[4])
+    wait_bytes(gb_full.at[pl.ds(0, NROW - 1)], send.at[5])
+    wait_bytes(ms.at[0], send.at[6])
+    wait_bytes(g_recv, send.at[7])
+    wait_bytes(g_recv, send.at[8])
+    wait_bytes(g_full.at[0], send.at[9])
+    wait_bytes(pb_recv, send.at[10])
+    wait_bytes(sq_row, send.at[11])
+    wait_bytes(sq_col, recv.at[12])
+    squares = sq_all[...] + jnp.sum(sq_col[...], axis=0)
+    b_out[...] = raw / jnp.sqrt(squares / ROWS_B + EPS)
+    wait_bytes(sq_col, send.at[12])
+
+
 VM = pl.BlockSpec(memory_space=pltpu.VMEM)
 SM = pl.BlockSpec(memory_space=pltpu.SMEM)
 ANY = pl.BlockSpec(memory_space=pl.ANY)
@@ -357,9 +574,7 @@
     return jax.ShapeDtypeStruct(dims, kind)
 
 
-def body(blocks, factor_b, factor_c, block_pos, block_count):
-    flat = blocks.reshape(SLOTS * BLK, WIDE)
-    place = block_pos.T
+def three_kernels(place, block_count, flat, factor_b, factor_c):
     vm, dma = pltpu.VMEM, pltpu.SemaphoreType.DMA
     gram_b, m16, ms, g = pl.pallas_call(
         kernel_a,
@@ -375,7 +590,7 @@
             vm((NROW, SHARE_G, R), F32), vm((NROW - 1, SHARE_G, R), F32), vm((2, NROW, SHARE_G, R), F32),
             dma((10,)), dma((10,)),
         ],
-        compiler_params=pltpu.CompilerParams(collective_id=0, has_side_effects=True),
+        compiler_params=pltpu.CompilerParams(collective_id=1, has_side_effects=True),
     )(place, block_count, flat, factor_b, factor_c)
     hat_a, lhs, inv = pl.pallas_call(
         kernel_b,
@@ -397,9 +612,35 @@
             vm((1, R), F32), vm((NROW - 1, 1, R), F32), vm((1, R), F32), vm((NCOL - 1, 1, R), F32),
             dma((3,)), dma((3,)),
         ],
-        compiler_params=pltpu.CompilerParams(collective_id=1, has_side_effects=True),
+        compiler_params=pltpu.CompilerParams(collective_id=2, has_side_effects=True),
     )(flat, factor_c, lhs, inv)
     return hat_a, hat_b
+
+
+def body(blocks, factor_b, factor_c, block_pos, block_count):
+    args = (block_pos.T, block_count, blocks.reshape(SLOTS * BLK, WIDE), factor_b, factor_c)
+    vm, dma = pltpu.VMEM, pltpu.SemaphoreType.DMA
+    hat_a, hat_b, worst = pl.pallas_call(
+        kernel_m,
+        name="sweep",
+        out_shape=(shape((SHARE_A, R)), shape((SHARE_B, R)), shape((8, 128))),
+        in_specs=[SM, SM, ANY, VM, VM],
+        out_specs=[VM] * 3,
+        scratch_shapes=[
+            vm((SLAB_A, WIDE), BF16), dma((NCH,)), vm((R, R), F32), vm((CHUNK, JBD * R), BF16), vm((SLAB_A, JBD * R), F32),
+            vm((R, R), F32), vm((NCOL, 1, R), F32), vm((NCOL - 1, 1, R), F32), vm((NCOL, 1, R), F32), vm((NROW, 32, R), F32),
+            vm((2, CHIPS, SHARE_A, R), F32), vm((CHIPS, SHARE_A, R), F32), vm((CHIPS, SHARE_A, R), BF16),
+            vm((CHIPS - 1, SHARE_A, R), BF16), vm((2, CHIPS, SHARE_A, R), BF16), vm((SHARE_A, R), F32),
+            vm((NROW, SHARE_G, R), F32), vm((NROW - 1, SHARE_G, R), F32), vm((2, NROW, SHARE_G, R), F32),
+            vm((R, R), F32), vm((R, R), F32), vm((SLAB_A, R), BF16), vm((R, SLAB_A), F32), vm((JBD * R, SLAB_A), BF16),
+            vm((JBD * R, CHUNK), F32), vm((JBD * R, BLK), F32),
+            vm((NROW, SHARE_B, R), BF16), vm((NROW - 1, SHARE_B, R), BF16),
+            vm((1, R), F32), vm((NROW - 1, 1, R), F32), vm((1, R), F32), vm((NCOL - 1, 1, R), F32),
+            dma((13,)), dma((13,)),
+        ],
+        compiler_params=pltpu.CompilerParams(collective_id=0, has_side_effects=True),
+    )(*args)
+    return lax.cond(worst[0, 0] <= 1e-3, lambda: (hat_a, hat_b), lambda: three_kernels(*args))
 
 
 def solution(mesh):

time: 93.8 us -> 150 us (1.60)
  Pallas kernels: 90.9 us -> 145 us
    pallas_call x3 -> x4, Pallas kernels: 90.9 us -> 145 us  [the longest x1 61 us: body(): pl.pallas_call(kernel_m, name='sweep', out_shape=(shape((SHARE_A, R)), sh...]
where the time goes in v3:
time: 150 us
  Pallas kernels  145 us (97%)
  local copies, waits for them, and re-layouts  2.43 us (2%)
  between operations  2.04 us (1%)
    pallas_call x1, Pallas kernels, body(): pl.pallas_call(kernel_m, name='sweep', out_shape=(shape((SHARE_A, R)), sh...  61 us
    pallas_call x1, Pallas kernels, three_kernels(): pl.pallas_call(kernel_a, name='mode_one', out_shape=(shape((R, R)), shape...  36.7 us
    pallas_call x1, Pallas kernels, three_kernels(): pl.pallas_call(kernel_c, name='mode_two', out_shape=shape((SHARE_B, R)),...  26.7 us
    pallas_call x1, Pallas kernels, three_kernels(): pl.pallas_call(kernel_b, name='solve_two', out_shape=(shape((SHARE_A, R))...  20.5 us

profile of v3, /device:TPU:1, one launch (start us, length us, event | category | flops | bytes accessed | tf_op | source)
XLA Modules:
  0.0 149.7 jit_solution(15578229846658574141)
XLA Ops:
  0.6 0.0 copy-start
  0.6 0.0 copy-start.1
  0.7 0.0 copy-start.2
  1.4 61.0 %sweep.1 = (f32[16,256]{1,0:T(8,128)S(1)}, f32[32,256]{1,0:T(8,128)S(1)}, f32[8,128]{1,0:T(8,128)}) custom-call(s32[1,4]{1,0:T(1,128)} %bitcast.5, s32[1,1]{1,0:T(1,128)S(6)} %copy.15.cnt, bf16[512,8192]{1,0:T(8,128)(2,1)} %bitcast.3, f32[256,256]{1,0:T(8,128)} %b_ref.1, f32[64,256]{1,0:T(8,128)} %c_ref.1), custom_call_target="tpu_custom_call" | custom-call | tf_op jit(solution)/shard_map/sweep/pallas_call | solution.py:623
  62.3 1.2 slice.3
  64.2 0.0 copy-done
  64.2 0.0 copy-done.1
  64.2 0.0 copy-done.2
  64.2 84.3 %conditional.1 = ((f32[16,256]{1,0:T(8,128)S(1)}, f32[32,256]{1,0:T(8,128)S(1)})) conditional(s32[]{:T(128)} %bitcast.2, (s32[1,4]{1,0:T(1,128)S(1)}, s32[1,1]{1,0:T(1,128)}, bf16[512,8192]{1,0:T(8,128)(2,1)}, f32[256,256]{1,0:T(8,128)S(1)}, f32[64,256]{1,0:T(8,128)S(1)}) %tuple.27, (f32[16,256]{1,0:T(8,128)S(1)}, f32[32,256]{1,0:T(8,128)S(1)}) %tuple.15), branch_computations={%region_0.0_spmd, %region_1.0_spmd} | conditional | bytes 24 | solution.py:643
  64.4 36.7 %mode_one.1 = (f32[256,256]{1,0:T(8,128)}, f32[16,256]{1,0:T(8,128)}, bf16[512,256]{1,0:T(8,128)(2,1)}, f32[256,256]{1,0:T(8,128)}) custom-call(s32[1,4]{1,0:T(1,128)S(1)} %get-tuple-element.14.pos, s32[1,1]{1,0:T(1,128)} %get-tuple-element.15.cnt, bf16[512,8192]{1,0:T(8,128)(2,1)} %get-tuple-element.17.x_hbm, f32[256,256]{1,0:T(8,128)S(1)} %get-tuple-element.18.b_ref, ...), custom_call_target="tpu_custom_call" | custom-call | tf_op jit(solution)/shard_map/cond/branch_0_fun/mode_one/pallas_call | solution.py:579
  101.1 20.5 %solve_two.1 = (f32[16,256]{1,0:T(8,128)S(1)}, bf16[512,512]{1,0:T(8,128)(2,1)}, f32[256,256]{1,0:T(8,128)}) custom-call(s32[1,4]{1,0:T(1,128)S(1)} %get-tuple-element.14.pos, s32[1,1]{1,0:T(1,128)} %get-tuple-element.15.cnt, f32[64,256]{1,0:T(8,128)S(1)} %get-tuple-element.16.c_ref, f32[256,256]{1,0:T(8,128)} %get-tuple-element.19.gb_ref, ...), custom_call_target="tpu_custom_call" | custom-call | tf_op jit(solution)/shard_map/cond/branch_0_fun/solve_two/pallas_call | solution.py:595
  121.6 26.7 %mode_two.1 = f32[32,256]{1,0:T(8,128)S(1)} custom-call(bf16[512,8192]{1,0:T(8,128)(2,1)} %get-tuple-element.17.x_hbm, f32[64,256]{1,0:T(8,128)S(1)} %get-tuple-element.16.c_ref, bf16[512,512]{1,0:T(8,128)(2,1)} %get-tuple-element.24.lhs, f32[256,256]{1,0:T(8,128)} %get-tuple-element.25.inv_ref), custom_call_target="tpu_custom_call" | custom-call | tf_op jit(solution)/shard_map/cond/branch_0_fun/mode_two/pallas_call | solution.py:603
  148.5 0.6 copy.16
  149.1 0.6 copy.17
Async XLA Ops:
  0.6 63.6 %copy-start = (f32[64,256]{1,0:T(8,128)S(1)}, f32[64,256]{1,0:T(8,128)}, u32[]{:S(2)}) copy-start(f32[64,256]{1,0:T(8,128)} %c_ref.1) | copy-start | bytes 196612
  0.6 63.6 %copy-start.1 = (f32[256,256]{1,0:T(8,128)S(1)}, f32[256,256]{1,0:T(8,128)}, u32[]{:S(2)}) copy-start(f32[256,256]{1,0:T(8,128)} %b_ref.1) | copy-start | bytes 786436
  0.7 63.6 %copy-start.2 = (s32[4,1]{0,1:T(1,128)S(1)}, s32[4,1]{0,1:T(1,128)}, u32[]{:S(2)}) copy-start(s32[4,1]{0,1:T(1,128)} %param.10) | copy-start | bytes 52

commit v4 on v3

--- a/solution.py
+++ b/solution.py
@@ -352,6 +352,13 @@
     return jnp.dot(a.astype(BF16), b.astype(BF16), preferred_element_type=F32)
 
 
+def dot_three(a, b):
+    a_top, b_top = a.astype(BF16), b.astype(BF16)
+    a_rest, b_rest = (a - a_top.astype(F32)).astype(BF16), (b - b_top.astype(F32)).astype(BF16)
+    cross = jnp.dot(a_top, b_rest, preferred_element_type=F32) + jnp.dot(a_rest, b_top, preferred_element_type=F32)
+    return jnp.dot(a_top, b_top, preferred_element_type=F32) + cross
+
+
 def short_inverse(v):
     down, across = diagonals(v)
     down, across = 1.0 / jnp.sqrt(down), 1.0 / jnp.sqrt(across)
@@ -362,7 +369,7 @@
     res = unit - alpha * c
     x = alpha * (unit + res)
     x = x + low_dot(x, low_dot(res, res))
-    x = x + low_dot(x, unit - dot_hi(c, x))
+    x = x + low_dot(x, unit - dot_three(c, x))
     res = unit - dot_hi(c, x)
     worst = jnp.max(jnp.sum(jnp.abs(res), axis=0, keepdims=True), axis=1, keepdims=True)
     x = x + low_dot(x, res)
@@ -372,10 +379,10 @@
 def kernel_m(
     pos, cnt, x_hbm, b_ref, c_ref,
     a_out, b_out, worst_out,
-    x_v, x_sem, br, w_v, acc,
+    x_v, x_sem, br, w_even, w_odd, acc,
     gram, gb_part, gb_recv, gb_col, gb_full,
     part, pair_recv, half, m_recv, ms, m16, g_piece, g_recv, g_full,
-    gram_c, inv1, slab, turned, lhs, ct, acc2,
+    gram_c, inv1, slab, turned, lhs, ct, ones,
     pb, pb_recv, sq_piece, sq_row, sq_all, sq_col,
     send, recv,
 ):
@@ -408,29 +415,40 @@
     cr = c_ref[...].astype(BF16).astype(F32)
     acc[...] = jnp.zeros_like(acc)
 
-    def mode_one(ch, carry):
+    cb = cr.astype(BF16)
+
+    def build(ch, w):
         for jb in range(JBD):
             tile = br[pl.ds(pl.multiple_of(jb * BLK + ch * JPC, JPC), JPC), :]
             for j in range(JPC):
-                w_v[j * K:(j + 1) * K, jb * R:(jb + 1) * R] = (tile[j:j + 1, :] * cr).astype(BF16)
+                w[jb, j * K:(j + 1) * K, :] = jnp.broadcast_to(tile[j:j + 1, :].astype(BF16), (K, R)) * cb
+
+    def add(ch, w):
         x_copy(ch).wait()
-        acc[...] += jnp.dot(x_v[:, chunk(ch)], w_v[...], preferred_element_type=F32)
-        return carry
-
-    lax.fori_loop(0, NCH - 3, mode_one, 0)
+        for s in range(SLOTS):
+            rows = slice(s * BLK, (s + 1) * BLK)
+            acc[rows, :] += jnp.dot(x_v[rows, chunk(ch)], w[pos[0, s] & 1], preferred_element_type=F32)
+
+    def mode_one(pair, carry):
+        add(2 * pair, w_even)
+        build(2 * pair + 1, w_odd)
+        add(2 * pair + 1, w_odd)
+        build(lax.rem(2 * pair + 2, NCH), w_even)
+        return carry
+
+    build(0, w_even)
+    lax.fori_loop(0, NCH // 2 - 1, mode_one, 0)
     pl.semaphore_wait(barrier, partners)
     scatter("col", NCOL, gb_part, gb_recv, send.at[0], recv.at[0])
-    lax.fori_loop(NCH - 3, NCH, mode_one, 0)
+    lax.fori_loop(NCH // 2 - 1, NCH // 2, mode_one, 0)
 
     count = cnt[0, 0]
     for ib in range(IBD):
         total = jnp.zeros((BLK, R), F32)
         for s in range(SLOTS):
-            p = pos[0, s]
             live = jnp.where(count > s, 1.0, 0.0).astype(F32)
-            for jb in range(JBD):
-                keep = jnp.where(p == ib * JBD + jb, live, 0.0)
-                total += acc[s * BLK:(s + 1) * BLK, jb * R:(jb + 1) * R] * keep
+            keep = jnp.where(lax.shift_right_logical(pos[0, s], 1) == ib, live, 0.0)
+            total += acc[s * BLK:(s + 1) * BLK, :] * keep
         for t in range(BLK // SHARE_A):
             at = ib * (BLK // SHARE_A) + t
             part[at % 2, at // 2] = total[t * SHARE_A:(t + 1) * SHARE_A, :]
@@ -458,7 +476,8 @@
     for jb in range(JBD):
         for t in range(CHUNK // K):
             ct[jb * R:(jb + 1) * R, t * K:(t + 1) * K] = c_low
-    acc2[...] = jnp.zeros_like(acc2)
+    whose = lax.shift_right_logical(lax.broadcasted_iota(jnp.int32, (JPC, CHUNK), 1), 6)
+    ones[...] = jnp.where(whose == lax.broadcasted_iota(jnp.int32, (JPC, CHUNK), 0), 1.0, 0.0).astype(BF16)
     wait_bytes(gb_col.at[pl.ds(0, NCOL - 1)], recv.at[3])
     for i in range(32):
         gb_full[me_r, i:i + 1, :] = gb_col[i]
@@ -508,36 +527,44 @@
                 tile += turned[:, ib * BLK:(ib + 1) * BLK] * jnp.where(p == ib * JBD + jb, live, 0.0)
             lhs[jb * R:(jb + 1) * R, s * BLK:(s + 1) * BLK] = tile.astype(BF16)
 
-    def mode_two(ch, carry):
-        t = jnp.dot(lhs[...], x_v[:, chunk(ch)], preferred_element_type=F32)
-        t = (t * ct[...]).astype(BF16)
-        j = lax.shift_right_logical(lax.broadcasted_iota(jnp.int32, (CHUNK, BLK), 0), 6) + ch * JPC
-        ones = jnp.where(j == lax.broadcasted_iota(jnp.int32, (CHUNK, BLK), 1), 1.0, 0.0).astype(BF16)
-        acc2[...] += jnp.dot(t, ones, preferred_element_type=F32)
-        return carry
-
-    lax.fori_loop(0, NCH - 4, mode_two, 0)
+    def mode_two(group, carry):
+        for side in range(2):
+            ch = 2 * group + side
+            t = jnp.dot(lhs[...], x_v[:, chunk(ch)], preferred_element_type=F32)
+            t = (t * ct[...]).astype(BF16)
+            rows = lax.dot_general(ones[...], t, last, preferred_element_type=F32).astype(BF16)
+            for jb in range(JBD):
+                pb[jb * (NROW // 2) + group, side * JPC:(side + 1) * JPC, :] = rows[:, jb * R:(jb + 1) * R]
+        for jb in range(JBD):
+            to = jb * (NROW // 2) + group
+
+            @pl.when(to != me_r)
+            def _():
+                pltpu.make_async_remote_copy(
+                    src_ref=pb.at[to], dst_ref=pb_recv.at[lax.rem(to - me_r + NROW, NROW) - 1],
+                    send_sem=send.at[10], recv_sem=recv.at[10],
+                    device_id={"row": to}, device_id_type=MESH,
+                ).start()
+
+        return carry
+
+    lax.fori_loop(0, 2, mode_two, 0)
     wait_bytes(g_recv, recv.at[7])
     g_full[core, me_r] = g_piece[me_r] + jnp.sum(g_recv[...], axis=0)
     gather("row", NROW, g_full.at[core, me_r], send.at[8], recv.at[8])
-    lax.fori_loop(NCH - 4, NCH, mode_two, 0)
-    for jb in range(JBD):
-        rows = acc2[jb * R:(jb + 1) * R, :].T.astype(BF16)
-        for t in range(BLK // SHARE_B):
-            pb[jb * (BLK // SHARE_B) + t] = rows[t * SHARE_B:(t + 1) * SHARE_B, :]
+    lax.fori_loop(2, 4, mode_two, 0)
     wait_bytes(g_recv, recv.at[8])
     to_mate(g_full.at[core], g_full.at[core], 9)
-    scatter("row", NROW, pb, pb_recv, send.at[10], recv.at[10])
 
     wait_bytes(g_full.at[0], recv.at[9])
     solved = inv1[...]
-    gram_a = dot_hi(dot_hi(solved, g_full[...].reshape(R, R)), solved)
+    gram_a = dot_three(dot_three(solved, g_full[...].reshape(R, R)), solved)
     down, across = diagonals(gram_a)
     down = 1.0 / jnp.sqrt(down / ROWS_A + EPS)
     across = 1.0 / jnp.sqrt(across / ROWS_A + EPS)
     a_out[...] = m16[...] * across
     inv2, worst_two = short_inverse(gram_a * down * across * gram_c[...])
-    worst_out[...] = jnp.full((8, 128), 1.0, F32) * jnp.maximum(worst_one, worst_two)
+    worst_out[...] = jnp.maximum(worst_one, worst_two)
 
     wait_bytes(pb_recv, recv.at[10])
     m2 = (pb[me_r].astype(F32) + jnp.sum(pb_recv[...].astype(F32), axis=0)) * across
@@ -623,17 +650,18 @@
     hat_a, hat_b, worst = pl.pallas_call(
         kernel_m,
         name="sweep",
-        out_shape=(shape((SHARE_A, R)), shape((SHARE_B, R)), shape((8, 128))),
+        out_shape=(shape((SHARE_A, R)), shape((SHARE_B, R)), shape((1, 1))),
         in_specs=[SM, SM, ANY, VM, VM],
         out_specs=[VM] * 3,
         scratch_shapes=[
-            vm((SLAB_A, WIDE), BF16), dma((NCH,)), vm((R, R), F32), vm((CHUNK, JBD * R), BF16), vm((SLAB_A, JBD * R), F32),
+            vm((SLAB_A, WIDE), BF16), dma((NCH,)), vm((R, R), F32), vm((JBD, CHUNK, R), BF16),
+            vm((JBD, CHUNK, R), BF16), vm((SLAB_A, R), F32),
             vm((R, R), F32), vm((NCOL, 1, R), F32), vm((NCOL - 1, 1, R), F32), vm((NCOL, 1, R), F32), vm((NROW, 32, R), F32),
             vm((2, CHIPS, SHARE_A, R), F32), vm((CHIPS, SHARE_A, R), F32), vm((CHIPS, SHARE_A, R), BF16),
             vm((CHIPS - 1, SHARE_A, R), BF16), vm((2, CHIPS, SHARE_A, R), BF16), vm((SHARE_A, R), F32),
             vm((NROW, SHARE_G, R), F32), vm((NROW - 1, SHARE_G, R), F32), vm((2, NROW, SHARE_G, R), F32),
             vm((R, R), F32), vm((R, R), F32), vm((SLAB_A, R), BF16), vm((R, SLAB_A), F32), vm((JBD * R, SLAB_A), BF16),
-            vm((JBD * R, CHUNK), F32), vm((JBD * R, BLK), F32),
+            vm((JBD * R, CHUNK), F32), vm((JPC, CHUNK), BF16),
             vm((NROW, SHARE_B, R), BF16), vm((NROW - 1, SHARE_B, R), BF16),
             vm((1, R), F32), vm((NROW - 1, 1, R), F32), vm((1, R), F32), vm((NCOL - 1, 1, R), F32),
             dma((13,)), dma((13,)),

time: 150 us -> 146 us (0.973)
  Pallas kernels: 145 us -> 142 us
    pallas_call x1, Pallas kernels: 61 us -> 58.3 us  [body(): pl.pallas_call(kernel_m, name='sweep', out_shape=(shape((SHARE_A, R)), sh...]
where the time goes in v4:
time: 146 us; the launch traced here: 145 us
  Pallas kernels  142 us (97%)
  between operations  2.07 us (1%)
    pallas_call x1, Pallas kernels, body(): pl.pallas_call(kernel_m, name='sweep', out_shape=(shape((SHARE_A, R)), sh...  58.3 us
    pallas_call x1, Pallas kernels, three_kernels(): pl.pallas_call(kernel_a, name='mode_one', out_shape=(shape((R, R)), shape...  37.6 us
    pallas_call x1, Pallas kernels, three_kernels(): pl.pallas_call(kernel_c, name='mode_two', out_shape=shape((SHARE_B, R)),...  25.2 us
    pallas_call x1, Pallas kernels, three_kernels(): pl.pallas_call(kernel_b, name='solve_two', out_shape=(shape((SHARE_A, R))...  20.5 us

profile of v4, /device:TPU:1, one launch (start us, length us, event | category | flops | bytes accessed | tf_op | source)
XLA Modules:
  0.0 145.3 jit_solution(3574790057864961666)
XLA Ops:
  0.6 0.0 copy-start
  0.6 0.0 copy-start.1
  0.7 0.0 copy-start.2
  1.4 58.3 %sweep.1 = (f32[16,256]{1,0:T(8,128)S(1)}, f32[32,256]{1,0:T(8,128)S(1)}, f32[1,1]{1,0:T(1,128)}) custom-call(s32[1,4]{1,0:T(1,128)} %bitcast.5, s32[1,1]{1,0:T(1,128)S(6)} %copy.15.cnt, bf16[512,8192]{1,0:T(8,128)(2,1)} %bitcast.3, f32[256,256]{1,0:T(8,128)} %b_ref.1, f32[64,256]{1,0:T(8,128)} %c_ref.1), custom_call_target="tpu_custom_call" | custom-call | tf_op jit(solution)/shard_map/sweep/pallas_call | solution.py:650
  60.4 0.0 copy-done
  60.4 0.0 copy-done.1
  60.4 0.0 copy-done.2
  60.4 83.7 %conditional.1 = ((f32[16,256]{1,0:T(8,128)S(1)}, f32[32,256]{1,0:T(8,128)S(1)})) conditional(s32[]{:T(128)} %bitcast.2, (s32[1,4]{1,0:T(1,128)S(1)}, s32[1,1]{1,0:T(1,128)}, bf16[512,8192]{1,0:T(8,128)(2,1)}, f32[256,256]{1,0:T(8,128)S(1)}, f32[64,256]{1,0:T(8,128)S(1)}) %tuple.27, (f32[16,256]{1,0:T(8,128)S(1)}, f32[32,256]{1,0:T(8,128)S(1)}) %tuple.15), branch_computations={%region_0.0_spmd, %region_1.0_spmd} | conditional | bytes 24 | solution.py:671
  60.6 37.6 %mode_one.1 = (f32[256,256]{1,0:T(8,128)}, f32[16,256]{1,0:T(8,128)}, bf16[512,256]{1,0:T(8,128)(2,1)}, f32[256,256]{1,0:T(8,128)}) custom-call(s32[1,4]{1,0:T(1,128)S(1)} %get-tuple-element.14.pos, s32[1,1]{1,0:T(1,128)} %get-tuple-element.15.cnt, bf16[512,8192]{1,0:T(8,128)(2,1)} %get-tuple-element.17.x_hbm, f32[256,256]{1,0:T(8,128)S(1)} %get-tuple-element.18.b_ref, ...), custom_call_target="tpu_custom_call" | custom-call | tf_op jit(solution)/shard_map/cond/branch_0_fun/mode_one/pallas_call | solution.py:606
  98.2 20.5 %solve_two.1 = (f32[16,256]{1,0:T(8,128)S(1)}, bf16[512,512]{1,0:T(8,128)(2,1)}, f32[256,256]{1,0:T(8,128)}) custom-call(s32[1,4]{1,0:T(1,128)S(1)} %get-tuple-element.14.pos, s32[1,1]{1,0:T(1,128)} %get-tuple-element.15.cnt, f32[64,256]{1,0:T(8,128)S(1)} %get-tuple-element.16.c_ref, f32[256,256]{1,0:T(8,128)} %get-tuple-element.19.gb_ref, ...), custom_call_target="tpu_custom_call" | custom-call | tf_op jit(solution)/shard_map/cond/branch_0_fun/solve_two/pallas_call | solution.py:622
  118.7 25.2 %mode_two.1 = f32[32,256]{1,0:T(8,128)S(1)} custom-call(bf16[512,8192]{1,0:T(8,128)(2,1)} %get-tuple-element.17.x_hbm, f32[64,256]{1,0:T(8,128)S(1)} %get-tuple-element.16.c_ref, bf16[512,512]{1,0:T(8,128)(2,1)} %get-tuple-element.24.lhs, f32[256,256]{1,0:T(8,128)} %get-tuple-element.25.inv_ref), custom_call_target="tpu_custom_call" | custom-call | tf_op jit(solution)/shard_map/cond/branch_0_fun/mode_two/pallas_call | solution.py:630
  144.1 0.6 copy.16
  144.7 0.6 copy.17
Async XLA Ops:
  0.6 59.7 %copy-start = (f32[64,256]{1,0:T(8,128)S(1)}, f32[64,256]{1,0:T(8,128)}, u32[]{:S(2)}) copy-start(f32[64,256]{1,0:T(8,128)} %c_ref.1) | copy-start | bytes 196612
  0.6 59.7 %copy-start.1 = (f32[256,256]{1,0:T(8,128)S(1)}, f32[256,256]{1,0:T(8,128)}, u32[]{:S(2)}) copy-start(f32[256,256]{1,0:T(8,128)} %b_ref.1) | copy-start | bytes 786436
  0.7 59.7 %copy-start.2 = (s32[4,1]{0,1:T(1,128)S(1)}, s32[4,1]{0,1:T(1,128)}, u32[]{:S(2)}) copy-start(s32[4,1]{0,1:T(1,128)} %param.10) | copy-start | bytes 52

commit v5 on v4

--- a/solution.py
+++ b/solution.py
@@ -23,6 +23,7 @@
 SHARE_B = SLAB_B // NROW
 CHIPS = NCOL // 2
 SHARE_G = BLK // NROW
+PLANE = NROW * 4
 ROWS_A = SLAB_A * NROW
 ROWS_B = SLAB_B * NCOL
 EPS = 1e-06
@@ -359,7 +360,7 @@
     return jnp.dot(a_top, b_top, preferred_element_type=F32) + cross
 
 
-def short_inverse(v):
+def first_half(v):
     down, across = diagonals(v)
     down, across = 1.0 / jnp.sqrt(down), 1.0 / jnp.sqrt(across)
     unit = jnp.where(eye(), 1.0, 0.0)
@@ -369,6 +370,11 @@
     res = unit - alpha * c
     x = alpha * (unit + res)
     x = x + low_dot(x, low_dot(res, res))
+    return c, x, down, across
+
+
+def second_half(c, x, down, across):
+    unit = jnp.where(eye(), 1.0, 0.0)
     x = x + low_dot(x, unit - dot_three(c, x))
     res = unit - dot_hi(c, x)
     worst = jnp.max(jnp.sum(jnp.abs(res), axis=0, keepdims=True), axis=1, keepdims=True)
@@ -404,7 +410,19 @@
 
     for ch in range(NCH):
         x_copy(ch).start()
-    barrier, partners = greet((("col", NCOL), ("row", NROW)))
+    barrier, partners = greet((("col", NCOL),))
+
+    def in_plane(k):
+        at = lax.rem(me_r * 4 + lax.rem(me_c, 4) + k, PLANE)
+        return at // 4, me_c // 4 * 4 + lax.rem(at, 4)
+
+    def greet_plane(k, carry):
+        row, col = in_plane(k)
+        pl.semaphore_signal(barrier, inc=1, device_id={"row": row, "col": col}, device_id_type=MESH)
+        return carry
+
+    lax.fori_loop(1, PLANE, greet_plane, 0)
+    partners += PLANE - 1
 
     b = b_ref[...]
     gram[...] = dot_hi(b.T, b)
@@ -479,9 +497,9 @@
     whose = lax.shift_right_logical(lax.broadcasted_iota(jnp.int32, (JPC, CHUNK), 1), 6)
     ones[...] = jnp.where(whose == lax.broadcasted_iota(jnp.int32, (JPC, CHUNK), 0), 1.0, 0.0).astype(BF16)
     wait_bytes(gb_col.at[pl.ds(0, NCOL - 1)], recv.at[3])
-    for i in range(32):
-        gb_full[me_r, i:i + 1, :] = gb_col[i]
-    gather("row", NROW, gb_full.at[me_r], send.at[5], recv.at[5])
+    for i in range(16):
+        gb_full[core, me_r, i:i + 1, :] = gb_col[core * 16 + i]
+    gather("row", NROW, gb_full.at[core, me_r], send.at[5], recv.at[5])
 
     wait_bytes(m_recv, recv.at[2])
     mine = part[core, chip] + pair_recv[chip] + jnp.sum(m_recv[...].astype(F32), axis=0)
@@ -497,10 +515,15 @@
 
     lax.fori_loop(1, CHIPS, from_chip, 0)
 
-    wait_bytes(gb_full.at[pl.ds(0, NROW - 1)], recv.at[5])
-    solved, worst_one = short_inverse(gb_full[...].reshape(R, R) * gram_c[...])
-    inv1[...] = solved
-    m16[...] = dot_hi(mine, solved)
+    wait_bytes(gb_full.at[0, pl.ds(0, NROW - 1)], recv.at[5])
+    to_mate(gb_full.at[core], gb_full.at[core], 13)
+    m16[...] = mine
+    wait_bytes(gb_full.at[0], recv.at[13])
+    for at in range(R // 16):
+        gram[at * 16:(at + 1) * 16, :] = gb_full[at % 2, at // 2]
+    c_one, x_one, down_one, across_one = first_half(gram[...] * gram_c[...])
+    turned[:, :R] = c_one
+    turned[:, R:] = x_one
 
     wait_bytes(m_recv, recv.at[4])
     to_mate(ms.at[core], ms.at[core], 6)
@@ -512,6 +535,8 @@
     g_piece[...] = gram[pl.ds(pl.multiple_of(core * BLK, BLK), BLK), :].reshape(NROW, SHARE_G, R)
     scatter("row", NROW, g_piece, g_recv, send.at[7], recv.at[7])
 
+    solved, worst_one = second_half(turned[:, :R], turned[:, R:], down_one, across_one)
+    inv1[...] = solved
     top = inv1[...].astype(BF16)
     rest = (inv1[...] - top.astype(F32)).astype(BF16)
     last = (((1,), (1,)), ((), ()))
@@ -562,34 +587,52 @@
     down, across = diagonals(gram_a)
     down = 1.0 / jnp.sqrt(down / ROWS_A + EPS)
     across = 1.0 / jnp.sqrt(across / ROWS_A + EPS)
-    a_out[...] = m16[...] * across
-    inv2, worst_two = short_inverse(gram_a * down * across * gram_c[...])
+    a_out[...] = dot_three(m16[...], solved) * across
+    inv2, worst_two = second_half(*first_half(gram_a * down * across * gram_c[...]))
     worst_out[...] = jnp.maximum(worst_one, worst_two)
 
     wait_bytes(pb_recv, recv.at[10])
     m2 = (pb[me_r].astype(F32) + jnp.sum(pb_recv[...].astype(F32), axis=0)) * across
     raw = dot_hi(m2, inv2)
     sq_piece[...] = jnp.sum(raw * raw, axis=0, keepdims=True)
-    spread("row", NROW, sq_piece, sq_row, send.at[11], recv.at[11])
-    wait_bytes(sq_row, recv.at[11])
-    sq_all[...] = sq_piece[...] + jnp.sum(sq_row[...], axis=0)
-    spread("col", NCOL, sq_all, sq_col, send.at[12], recv.at[12])
+
+    def to_plane(k, carry):
+        row, col = in_plane(k)
+        pltpu.make_async_remote_copy(
+            src_ref=sq_piece, dst_ref=sq_col.at[k - 1], send_sem=send.at[11], recv_sem=recv.at[11],
+            device_id={"row": row, "col": col}, device_id_type=MESH,
+        ).start()
+        return carry
+
+    lax.fori_loop(1, PLANE, to_plane, 0)
+    wait_bytes(sq_col, recv.at[11])
+    sq_all[...] = sq_piece[...] + jnp.sum(sq_col[...], axis=0)
+
+    def to_planes(k, carry):
+        pltpu.make_async_remote_copy(
+            src_ref=sq_all, dst_ref=sq_row.at[k - 1], send_sem=send.at[12], recv_sem=recv.at[12],
+            device_id={"col": lax.rem(me_c + k * 4, NCOL)}, device_id_type=MESH,
+        ).start()
+        return carry
+
+    lax.fori_loop(1, NCOL // 4, to_planes, 0)
     wait_bytes(gb_recv, send.at[0])
     wait_bytes(pair_recv, send.at[1])
     wait_bytes(m_recv, send.at[2])
     wait_bytes(gb_col.at[pl.ds(0, NCOL - 1)], send.at[3])
     wait_bytes(m_recv, send.at[4])
-    wait_bytes(gb_full.at[pl.ds(0, NROW - 1)], send.at[5])
+    wait_bytes(gb_full.at[0, pl.ds(0, NROW - 1)], send.at[5])
+    wait_bytes(gb_full.at[0], send.at[13])
     wait_bytes(ms.at[0], send.at[6])
     wait_bytes(g_recv, send.at[7])
     wait_bytes(g_recv, send.at[8])
     wait_bytes(g_full.at[0], send.at[9])
     wait_bytes(pb_recv, send.at[10])
-    wait_bytes(sq_row, send.at[11])
-    wait_bytes(sq_col, recv.at[12])
-    squares = sq_all[...] + jnp.sum(sq_col[...], axis=0)
+    wait_bytes(sq_col, send.at[11])
+    wait_bytes(sq_row, recv.at[12])
+    squares = sq_all[...] + jnp.sum(sq_row[...], axis=0)
     b_out[...] = raw / jnp.sqrt(squares / ROWS_B + EPS)
-    wait_bytes(sq_col, send.at[12])
+    wait_bytes(sq_row, send.at[12])
 
 
 VM = pl.BlockSpec(memory_space=pltpu.VMEM)
@@ -656,7 +699,7 @@
         scratch_shapes=[
             vm((SLAB_A, WIDE), BF16), dma((NCH,)), vm((R, R), F32), vm((JBD, CHUNK, R), BF16),
             vm((JBD, CHUNK, R), BF16), vm((SLAB_A, R), F32),
-            vm((R, R), F32), vm((NCOL, 1, R), F32), vm((NCOL - 1, 1, R), F32), vm((NCOL, 1, R), F32), vm((NROW, 32, R), F32),
+            vm((R, R), F32), vm((NCOL, 1, R), F32), vm((NCOL - 1, 1, R), F32), vm((NCOL, 1, R), F32), vm((2, NROW, 16, R), F32),
             vm((2, CHIPS, SHARE_A, R), F32), vm((CHIPS, SHARE_A, R), F32), vm((CHIPS, SHARE_A, R), BF16),
             vm((CHIPS - 1, SHARE_A, R), BF16), vm((2, CHIPS, SHARE_A, R), BF16), vm((SHARE_A, R), F32),
             vm((NROW, SHARE_G, R), F32), vm((NROW - 1, SHARE_G, R), F32), vm((2, NROW, SHARE_G, R), F32),
@@ -664,7 +707,7 @@
             vm((JBD * R, CHUNK), F32), vm((JPC, CHUNK), BF16),
             vm((NROW, SHARE_B, R), BF16), vm((NROW - 1, SHARE_B, R), BF16),
             vm((1, R), F32), vm((NROW - 1, 1, R), F32), vm((1, R), F32), vm((NCOL - 1, 1, R), F32),
-            dma((13,)), dma((13,)),
+            dma((14,)), dma((14,)),
         ],
         compiler_params=pltpu.CompilerParams(collective_id=0, has_side_effects=True),
     )(*args)

time: 146 us -> 145 us (level)
  no operation moved by 1% of the time
where the time goes in v5:
time: 145 us
  Pallas kernels  141 us (97%)
  between operations  2.07 us (1%)
    pallas_call x1, Pallas kernels, body(): pl.pallas_call(kernel_m, name='sweep', out_shape=(shape((SHARE_A, R)), sh...  57.1 us
    pallas_call x1, Pallas kernels, three_kernels(): pl.pallas_call(kernel_a, name='mode_one', out_shape=(shape((R, R)), shape...  38 us
    pallas_call x1, Pallas kernels, three_kernels(): pl.pallas_call(kernel_c, name='mode_two', out_shape=shape((SHARE_B, R)),...  25.4 us
    pallas_call x1, Pallas kernels, three_kernels(): pl.pallas_call(kernel_b, name='solve_two', out_shape=(shape((SHARE_A, R))...  20.5 us

profile of v5, /device:TPU:1, one launch (start us, length us, event | category | flops | bytes accessed | tf_op | source)
XLA Modules:
  0.0 144.7 jit_solution(4403140221598119803)
XLA Ops:
  0.6 0.0 copy-start
  0.6 0.0 copy-start.1
  0.7 0.0 copy-start.2
  1.4 57.1 %sweep.1 = (f32[16,256]{1,0:T(8,128)S(1)}, f32[32,256]{1,0:T(8,128)S(1)}, f32[1,1]{1,0:T(1,128)}) custom-call(s32[1,4]{1,0:T(1,128)} %bitcast.5, s32[1,1]{1,0:T(1,128)S(6)} %copy.15.cnt, bf16[512,8192]{1,0:T(8,128)(2,1)} %bitcast.3, f32[256,256]{1,0:T(8,128)} %b_ref.1, f32[64,256]{1,0:T(8,128)} %c_ref.1), custom_call_target="tpu_custom_call" | custom-call | tf_op jit(solution)/shard_map/sweep/pallas_call | solution.py:693
  59.1 0.0 copy-done
  59.1 0.0 copy-done.1
  59.1 0.0 copy-done.2
  59.1 84.4 %conditional.1 = ((f32[16,256]{1,0:T(8,128)S(1)}, f32[32,256]{1,0:T(8,128)S(1)})) conditional(s32[]{:T(128)} %bitcast.2, (s32[1,4]{1,0:T(1,128)S(1)}, s32[1,1]{1,0:T(1,128)}, bf16[512,8192]{1,0:T(8,128)(2,1)}, f32[256,256]{1,0:T(8,128)S(1)}, f32[64,256]{1,0:T(8,128)S(1)}) %tuple.27, (f32[16,256]{1,0:T(8,128)S(1)}, f32[32,256]{1,0:T(8,128)S(1)}) %tuple.15), branch_computations={%region_0.0_spmd, %region_1.0_spmd} | conditional | bytes 24 | solution.py:714
  59.3 38.0 %mode_one.1 = (f32[256,256]{1,0:T(8,128)}, f32[16,256]{1,0:T(8,128)}, bf16[512,256]{1,0:T(8,128)(2,1)}, f32[256,256]{1,0:T(8,128)}) custom-call(s32[1,4]{1,0:T(1,128)S(1)} %get-tuple-element.14.pos, s32[1,1]{1,0:T(1,128)} %get-tuple-element.15.cnt, bf16[512,8192]{1,0:T(8,128)(2,1)} %get-tuple-element.17.x_hbm, f32[256,256]{1,0:T(8,128)S(1)} %get-tuple-element.18.b_ref, ...), custom_call_target="tpu_custom_call" | custom-call | tf_op jit(solution)/shard_map/cond/branch_0_fun/mode_one/pallas_call | solution.py:649
  97.3 20.5 %solve_two.1 = (f32[16,256]{1,0:T(8,128)S(1)}, bf16[512,512]{1,0:T(8,128)(2,1)}, f32[256,256]{1,0:T(8,128)}) custom-call(s32[1,4]{1,0:T(1,128)S(1)} %get-tuple-element.14.pos, s32[1,1]{1,0:T(1,128)} %get-tuple-element.15.cnt, f32[64,256]{1,0:T(8,128)S(1)} %get-tuple-element.16.c_ref, f32[256,256]{1,0:T(8,128)} %get-tuple-element.19.gb_ref, ...), custom_call_target="tpu_custom_call" | custom-call | tf_op jit(solution)/shard_map/cond/branch_0_fun/solve_two/pallas_call | solution.py:665
  117.8 25.4 %mode_two.1 = f32[32,256]{1,0:T(8,128)S(1)} custom-call(bf16[512,8192]{1,0:T(8,128)(2,1)} %get-tuple-element.17.x_hbm, f32[64,256]{1,0:T(8,128)S(1)} %get-tuple-element.16.c_ref, bf16[512,512]{1,0:T(8,128)(2,1)} %get-tuple-element.24.lhs, f32[256,256]{1,0:T(8,128)} %get-tuple-element.25.inv_ref), custom_call_target="tpu_custom_call" | custom-call | tf_op jit(solution)/shard_map/cond/branch_0_fun/mode_two/pallas_call | solution.py:673
  143.5 0.6 copy.16
  144.1 0.6 copy.17
Async XLA Ops:
  0.6 58.5 %copy-start = (f32[64,256]{1,0:T(8,128)S(1)}, f32[64,256]{1,0:T(8,128)}, u32[]{:S(2)}) copy-start(f32[64,256]{1,0:T(8,128)} %c_ref.1) | copy-start | bytes 196612
  0.6 58.5 %copy-start.1 = (f32[256,256]{1,0:T(8,128)S(1)}, f32[256,256]{1,0:T(8,128)}, u32[]{:S(2)}) copy-start(f32[256,256]{1,0:T(8,128)} %b_ref.1) | copy-start | bytes 786436
  0.7 58.5 %copy-start.2 = (s32[4,1]{0,1:T(1,128)S(1)}, s32[4,1]{0,1:T(1,128)}, u32[]{:S(2)}) copy-start(s32[4,1]{0,1:T(1,128)} %param.10) | copy-start | bytes 52

commit v6 on v5

--- a/solution.py
+++ b/solution.py
@@ -24,6 +24,7 @@
 CHIPS = NCOL // 2
 SHARE_G = BLK // NROW
 PLANE = NROW * 4
+PIECE_G = SHARE_G * 3 // 2
 ROWS_A = SLAB_A * NROW
 ROWS_B = SLAB_B * NCOL
 EPS = 1e-06
@@ -469,23 +470,27 @@
             total += acc[s * BLK:(s + 1) * BLK, :] * keep
         for t in range(BLK // SHARE_A):
             at = ib * (BLK // SHARE_A) + t
-            part[at % 2, at // 2] = total[t * SHARE_A:(t + 1) * SHARE_A, :]
-
-    to_mate(part.at[1 - core], pair_recv, 1)
+            for side in range(2):
+                part[side, at % 2, at // 2] = total[t * SHARE_A:(t + 1) * SHARE_A, side * BLK:(side + 1) * BLK]
+
+    for side in range(2):
+        to_mate(part.at[side, 1 - core], pair_recv.at[side], (1, 14)[side])
     c = c_ref[...]
     gram_c[...] = dot_hi(c.T, c)
-    wait_bytes(pair_recv, recv.at[1])
-    half[...] = (part[core] + pair_recv[...]).astype(BF16)
-
-    def to_chip(k, carry):
+
+    def to_chip(side, k, carry):
         d = lax.rem(chip + k, CHIPS)
-        pltpu.make_async_remote_copy(
-            src_ref=half.at[d], dst_ref=m_recv.at[k - 1], send_sem=send.at[2], recv_sem=recv.at[2],
+        n = (2, 15)[side]
+        pltpu.make_async_remote_copy(
+            src_ref=half.at[side, d], dst_ref=m_recv.at[side, k - 1], send_sem=send.at[n], recv_sem=recv.at[n],
             device_id={"col": d * 2 + core}, device_id_type=MESH,
         ).start()
         return carry
 
-    lax.fori_loop(1, CHIPS, to_chip, 0)
+    for side in range(2):
+        wait_bytes(pair_recv.at[side], recv.at[(1, 14)[side]])
+        half[side] = (part[side, core] + pair_recv[side]).astype(BF16)
+        lax.fori_loop(1, CHIPS, functools.partial(to_chip, side), 0)
 
     wait_bytes(gb_recv, recv.at[0])
     gb_col[me_c] = gb_part[me_c] + jnp.sum(gb_recv[...], axis=0)
@@ -496,28 +501,32 @@
             ct[jb * R:(jb + 1) * R, t * K:(t + 1) * K] = c_low
     whose = lax.shift_right_logical(lax.broadcasted_iota(jnp.int32, (JPC, CHUNK), 1), 6)
     ones[...] = jnp.where(whose == lax.broadcasted_iota(jnp.int32, (JPC, CHUNK), 0), 1.0, 0.0).astype(BF16)
+
+    def from_chip(side, k, carry):
+        piece = ms.at[side, core, chip]
+        n = (4, 16)[side]
+        pltpu.make_async_remote_copy(
+            src_ref=piece, dst_ref=piece, send_sem=send.at[n], recv_sem=recv.at[n],
+            device_id={"col": lax.rem(chip + k, CHIPS) * 2 + core}, device_id_type=MESH,
+        ).start()
+        return carry
+
+    def pass_on(side):
+        wait_bytes(m_recv.at[side], recv.at[(2, 15)[side]])
+        mine = part[side, core, chip] + pair_recv[side, chip] + jnp.sum(m_recv[side].astype(F32), axis=0)
+        ms[side, core, chip] = mine.astype(BF16)
+        lax.fori_loop(1, CHIPS, functools.partial(from_chip, side), 0)
+        m16[:, side * BLK:(side + 1) * BLK] = mine
+
+    pass_on(0)
     wait_bytes(gb_col.at[pl.ds(0, NCOL - 1)], recv.at[3])
     for i in range(16):
         gb_full[core, me_r, i:i + 1, :] = gb_col[core * 16 + i]
     gather("row", NROW, gb_full.at[core, me_r], send.at[5], recv.at[5])
-
-    wait_bytes(m_recv, recv.at[2])
-    mine = part[core, chip] + pair_recv[chip] + jnp.sum(m_recv[...].astype(F32), axis=0)
-    ms[core, chip] = mine.astype(BF16)
-
-    def from_chip(k, carry):
-        piece = ms.at[core, chip]
-        pltpu.make_async_remote_copy(
-            src_ref=piece, dst_ref=piece, send_sem=send.at[4], recv_sem=recv.at[4],
-            device_id={"col": lax.rem(chip + k, CHIPS) * 2 + core}, device_id_type=MESH,
-        ).start()
-        return carry
-
-    lax.fori_loop(1, CHIPS, from_chip, 0)
+    pass_on(1)
 
     wait_bytes(gb_full.at[0, pl.ds(0, NROW - 1)], recv.at[5])
     to_mate(gb_full.at[core], gb_full.at[core], 13)
-    m16[...] = mine
     wait_bytes(gb_full.at[0], recv.at[13])
     for at in range(R // 16):
         gram[at * 16:(at + 1) * 16, :] = gb_full[at % 2, at // 2]
@@ -525,14 +534,19 @@
     turned[:, :R] = c_one
     turned[:, R:] = x_one
 
-    wait_bytes(m_recv, recv.at[4])
-    to_mate(ms.at[core], ms.at[core], 6)
-    wait_bytes(ms.at[0], recv.at[6])
-    for at in range(NCOL):
-        slab[at * SHARE_A:(at + 1) * SHARE_A, :] = ms[at % 2, at // 2]
+    for side in range(2):
+        wait_bytes(m_recv.at[side], recv.at[(4, 16)[side]])
+        to_mate(ms.at[side, core], ms.at[side, core], (6, 17)[side])
+    for side in range(2):
+        wait_bytes(ms.at[side, 0], recv.at[(6, 17)[side]])
+        for at in range(NCOL):
+            slab[at * SHARE_A:(at + 1) * SHARE_A, side * BLK:(side + 1) * BLK] = ms[side, at % 2, at // 2]
 
     gram[...] = jnp.dot(slab[...].T, slab[...], preferred_element_type=F32)
-    g_piece[...] = gram[pl.ds(pl.multiple_of(core * BLK, BLK), BLK), :].reshape(NROW, SHARE_G, R)
+    own = jnp.where(core == 0, gram[:BLK, :BLK], gram[BLK:, BLK:])
+    cross = gram[pl.ds(pl.multiple_of(core * (BLK // 2), BLK // 2), BLK // 2), BLK:]
+    g_piece[:, :SHARE_G, :] = own.reshape(NROW, SHARE_G, BLK)
+    g_piece[:, SHARE_G:, :] = cross.reshape(NROW, SHARE_G // 2, BLK)
     scatter("row", NROW, g_piece, g_recv, send.at[7], recv.at[7])
 
     solved, worst_one = second_half(turned[:, :R], turned[:, R:], down_one, across_one)
@@ -583,7 +597,12 @@
 
     wait_bytes(g_full.at[0], recv.at[9])
     solved = inv1[...]
-    gram_a = dot_three(dot_three(solved, g_full[...].reshape(R, R)), solved)
+    for e in range(2):
+        gram[e * BLK:(e + 1) * BLK, e * BLK:(e + 1) * BLK] = g_full[e, :, :SHARE_G, :].reshape(BLK, BLK)
+        cross = g_full[e, :, SHARE_G:, :].reshape(BLK // 2, BLK)
+        gram[e * (BLK // 2):(e + 1) * (BLK // 2), BLK:] = cross
+    gram[BLK:, :BLK] = gram[:BLK, BLK:].T
+    gram_a = dot_three(dot_three(solved, gram[...]), solved)
     down, across = diagonals(gram_a)
     down = 1.0 / jnp.sqrt(down / ROWS_A + EPS)
     across = 1.0 / jnp.sqrt(across / ROWS_A + EPS)
@@ -617,13 +636,14 @@
 
     lax.fori_loop(1, NCOL // 4, to_planes, 0)
     wait_bytes(gb_recv, send.at[0])
-    wait_bytes(pair_recv, send.at[1])
-    wait_bytes(m_recv, send.at[2])
+    for side in range(2):
+        wait_bytes(pair_recv.at[side], send.at[(1, 14)[side]])
+        wait_bytes(m_recv.at[side], send.at[(2, 15)[side]])
+        wait_bytes(m_recv.at[side], send.at[(4, 16)[side]])
+        wait_bytes(ms.at[side, 0], send.at[(6, 17)[side]])
     wait_bytes(gb_col.at[pl.ds(0, NCOL - 1)], send.at[3])
-    wait_bytes(m_recv, send.at[4])
     wait_bytes(gb_full.at[0, pl.ds(0, NROW - 1)], send.at[5])
     wait_bytes(gb_full.at[0], send.at[13])
-    wait_bytes(ms.at[0], send.at[6])
     wait_bytes(g_recv, send.at[7])
     wait_bytes(g_recv, send.at[8])
     wait_bytes(g_full.at[0], send.at[9])
@@ -700,14 +720,14 @@
             vm((SLAB_A, WIDE), BF16), dma((NCH,)), vm((R, R), F32), vm((JBD, CHUNK, R), BF16),
             vm((JBD, CHUNK, R), BF16), vm((SLAB_A, R), F32),
             vm((R, R), F32), vm((NCOL, 1, R), F32), vm((NCOL - 1, 1, R), F32), vm((NCOL, 1, R), F32), vm((2, NROW, 16, R), F32),
-            vm((2, CHIPS, SHARE_A, R), F32), vm((CHIPS, SHARE_A, R), F32), vm((CHIPS, SHARE_A, R), BF16),
-            vm((CHIPS - 1, SHARE_A, R), BF16), vm((2, CHIPS, SHARE_A, R), BF16), vm((SHARE_A, R), F32),
-            vm((NROW, SHARE_G, R), F32), vm((NROW - 1, SHARE_G, R), F32), vm((2, NROW, SHARE_G, R), F32),
+            vm((2, 2, CHIPS, SHARE_A, BLK), F32), vm((2, CHIPS, SHARE_A, BLK), F32), vm((2, CHIPS, SHARE_A, BLK), BF16),
+            vm((2, CHIPS - 1, SHARE_A, BLK), BF16), vm((2, 2, CHIPS, SHARE_A, BLK), BF16), vm((SHARE_A, R), F32),
+            vm((NROW, PIECE_G, BLK), F32), vm((NROW - 1, PIECE_G, BLK), F32), vm((2, NROW, PIECE_G, BLK), F32),
             vm((R, R), F32), vm((R, R), F32), vm((SLAB_A, R), BF16), vm((R, SLAB_A), F32), vm((JBD * R, SLAB_A), BF16),
             vm((JBD * R, CHUNK), F32), vm((JPC, CHUNK), BF16),
             vm((NROW, SHARE_B, R), BF16), vm((NROW - 1, SHARE_B, R), BF16),
             vm((1, R), F32), vm((NROW - 1, 1, R), F32), vm((1, R), F32), vm((NCOL - 1, 1, R), F32),
-            dma((14,)), dma((14,)),
+            dma((18,)), dma((18,)),
         ],
         compiler_params=pltpu.CompilerParams(collective_id=0, has_side_effects=True),
     )(*args)

time: 145 us -> 144 us (level)
  no operation moved by 1% of the time
where the time goes in v6:
time: 144 us; the launch traced here: 143 us
  Pallas kernels  140 us (97%)
  between operations  2.07 us (1%)
    pallas_call x1, Pallas kernels, body(): pl.pallas_call(kernel_m, name='sweep', out_shape=(shape((SHARE_A, R)), sh...  56.1 us
    pallas_call x1, Pallas kernels, three_kernels(): pl.pallas_call(kernel_a, name='mode_one', out_shape=(shape((R, R)), shape...  38.1 us
    pallas_call x1, Pallas kernels, three_kernels(): pl.pallas_call(kernel_c, name='mode_two', out_shape=shape((SHARE_B, R)),...  25.1 us
    pallas_call x1, Pallas kernels, three_kernels(): pl.pallas_call(kernel_b, name='solve_two', out_shape=(shape((SHARE_A, R))...  20.5 us

profile of v6, /device:TPU:1, one launch (start us, length us, event | category | flops | bytes accessed | tf_op | source)
XLA Modules:
  0.0 143.4 jit_solution(13495186474982136174)
XLA Ops:
  0.6 0.0 copy-start
  0.6 0.0 copy-start.1
  0.7 0.0 copy-start.2
  1.4 56.1 %sweep.1 = (f32[16,256]{1,0:T(8,128)S(1)}, f32[32,256]{1,0:T(8,128)S(1)}, f32[1,1]{1,0:T(1,128)}) custom-call(s32[1,4]{1,0:T(1,128)} %bitcast.5, s32[1,1]{1,0:T(1,128)S(6)} %copy.15.cnt, bf16[512,8192]{1,0:T(8,128)(2,1)} %bitcast.3, f32[256,256]{1,0:T(8,128)} %b_ref.1, f32[64,256]{1,0:T(8,128)} %c_ref.1), custom_call_target="tpu_custom_call" | custom-call | tf_op jit(solution)/shard_map/sweep/pallas_call | solution.py:713
  58.1 0.0 copy-done
  58.1 0.0 copy-done.1
  58.1 0.0 copy-done.2
  58.1 84.0 %conditional.1 = ((f32[16,256]{1,0:T(8,128)S(1)}, f32[32,256]{1,0:T(8,128)S(1)})) conditional(s32[]{:T(128)} %bitcast.2, (s32[1,4]{1,0:T(1,128)S(1)}, s32[1,1]{1,0:T(1,128)}, bf16[512,8192]{1,0:T(8,128)(2,1)}, f32[256,256]{1,0:T(8,128)S(1)}, f32[64,256]{1,0:T(8,128)S(1)}) %tuple.27, (f32[16,256]{1,0:T(8,128)S(1)}, f32[32,256]{1,0:T(8,128)S(1)}) %tuple.15), branch_computations={%region_0.0_spmd, %region_1.0_spmd} | conditional | bytes 24 | solution.py:734
  58.3 38.1 %mode_one.1 = (f32[256,256]{1,0:T(8,128)}, f32[16,256]{1,0:T(8,128)}, bf16[512,256]{1,0:T(8,128)(2,1)}, f32[256,256]{1,0:T(8,128)}) custom-call(s32[1,4]{1,0:T(1,128)S(1)} %get-tuple-element.14.pos, s32[1,1]{1,0:T(1,128)} %get-tuple-element.15.cnt, bf16[512,8192]{1,0:T(8,128)(2,1)} %get-tuple-element.17.x_hbm, f32[256,256]{1,0:T(8,128)S(1)} %get-tuple-element.18.b_ref, ...), custom_call_target="tpu_custom_call" | custom-call | tf_op jit(solution)/shard_map/cond/branch_0_fun/mode_one/pallas_call | solution.py:669
  96.4 20.5 %solve_two.1 = (f32[16,256]{1,0:T(8,128)S(1)}, bf16[512,512]{1,0:T(8,128)(2,1)}, f32[256,256]{1,0:T(8,128)}) custom-call(s32[1,4]{1,0:T(1,128)S(1)} %get-tuple-element.14.pos, s32[1,1]{1,0:T(1,128)} %get-tuple-element.15.cnt, f32[64,256]{1,0:T(8,128)S(1)} %get-tuple-element.16.c_ref, f32[256,256]{1,0:T(8,128)} %get-tuple-element.19.gb_ref, ...), custom_call_target="tpu_custom_call" | custom-call | tf_op jit(solution)/shard_map/cond/branch_0_fun/solve_two/pallas_call | solution.py:685
  116.9 25.1 %mode_two.1 = f32[32,256]{1,0:T(8,128)S(1)} custom-call(bf16[512,8192]{1,0:T(8,128)(2,1)} %get-tuple-element.17.x_hbm, f32[64,256]{1,0:T(8,128)S(1)} %get-tuple-element.16.c_ref, bf16[512,512]{1,0:T(8,128)(2,1)} %get-tuple-element.24.lhs, f32[256,256]{1,0:T(8,128)} %get-tuple-element.25.inv_ref), custom_call_target="tpu_custom_call" | custom-call | tf_op jit(solution)/shard_map/cond/branch_0_fun/mode_two/pallas_call | solution.py:693
  142.2 0.6 copy.16
  142.8 0.6 copy.17
Async XLA Ops:
  0.6 57.5 %copy-start = (f32[64,256]{1,0:T(8,128)S(1)}, f32[64,256]{1,0:T(8,128)}, u32[]{:S(2)}) copy-start(f32[64,256]{1,0:T(8,128)} %c_ref.1) | copy-start | bytes 196612
  0.6 57.5 %copy-start.1 = (f32[256,256]{1,0:T(8,128)S(1)}, f32[256,256]{1,0:T(8,128)}, u32[]{:S(2)}) copy-start(f32[256,256]{1,0:T(8,128)} %b_ref.1) | copy-start | bytes 786436
  0.7 57.5 %copy-start.2 = (s32[4,1]{0,1:T(1,128)S(1)}, s32[4,1]{0,1:T(1,128)}, u32[]{:S(2)}) copy-start(s32[4,1]{0,1:T(1,128)} %param.10) | copy-start | bytes 52

commit v7 on v6

--- a/solution.py
+++ b/solution.py
@@ -350,6 +350,38 @@
     wait_bytes(sq_col, send.at[2])
 
 
+def far(n, count):
+    return count // 2 + (1 - 2 * lax.rem(n, 2)) * ((n + 1) // 2)
+
+
+def scatter_far(axis, count, src, dst, send, recv):
+    me = lax.axis_index(axis)
+
+    def one(n, carry):
+        k = far(n, count)
+        d = lax.rem(me + k, count)
+        pltpu.make_async_remote_copy(
+            src_ref=src.at[d], dst_ref=dst.at[k - 1], send_sem=send, recv_sem=recv,
+            device_id={axis: d}, device_id_type=MESH,
+        ).start()
+        return carry
+
+    lax.fori_loop(0, count - 1, one, 0)
+
+
+def gather_far(axis, count, piece, send, recv):
+    me = lax.axis_index(axis)
+
+    def one(n, carry):
+        pltpu.make_async_remote_copy(
+            src_ref=piece, dst_ref=piece, send_sem=send, recv_sem=recv,
+            device_id={axis: lax.rem(me + far(n, count), count)}, device_id_type=MESH,
+        ).start()
+        return carry
+
+    lax.fori_loop(0, count - 1, one, 0)
+
+
 def low_dot(a, b):
     return jnp.dot(a.astype(BF16), b.astype(BF16), preferred_element_type=F32)
 
@@ -377,7 +409,7 @@
 def second_half(c, x, down, across):
     unit = jnp.where(eye(), 1.0, 0.0)
     x = x + low_dot(x, unit - dot_three(c, x))
-    res = unit - dot_hi(c, x)
+    res = unit - dot_three(c, x)
     worst = jnp.max(jnp.sum(jnp.abs(res), axis=0, keepdims=True), axis=1, keepdims=True)
     x = x + low_dot(x, res)
     return x * down * across, worst
@@ -458,7 +490,7 @@
     build(0, w_even)
     lax.fori_loop(0, NCH // 2 - 1, mode_one, 0)
     pl.semaphore_wait(barrier, partners)
-    scatter("col", NCOL, gb_part, gb_recv, send.at[0], recv.at[0])
+    scatter_far("col", NCOL, gb_part, gb_recv, send.at[0], recv.at[0])
     lax.fori_loop(NCH // 2 - 1, NCH // 2, mode_one, 0)
 
     count = cnt[0, 0]
@@ -478,7 +510,8 @@
     c = c_ref[...]
     gram_c[...] = dot_hi(c.T, c)
 
-    def to_chip(side, k, carry):
+    def to_chip(side, at, carry):
+        k = far(at, CHIPS)
         d = lax.rem(chip + k, CHIPS)
         n = (2, 15)[side]
         pltpu.make_async_remote_copy(
@@ -490,11 +523,11 @@
     for side in range(2):
         wait_bytes(pair_recv.at[side], recv.at[(1, 14)[side]])
         half[side] = (part[side, core] + pair_recv[side]).astype(BF16)
-        lax.fori_loop(1, CHIPS, functools.partial(to_chip, side), 0)
+        lax.fori_loop(0, CHIPS - 1, functools.partial(to_chip, side), 0)
 
     wait_bytes(gb_recv, recv.at[0])
     gb_col[me_c] = gb_part[me_c] + jnp.sum(gb_recv[...], axis=0)
-    gather("col", NCOL, gb_col.at[me_c], send.at[3], recv.at[3])
+    gather_far("col", NCOL, gb_col.at[me_c], send.at[3], recv.at[3])
     c_low = cr.T
     for jb in range(JBD):
         for t in range(CHUNK // K):
@@ -502,7 +535,8 @@
     whose = lax.shift_right_logical(lax.broadcasted_iota(jnp.int32, (JPC, CHUNK), 1), 6)
     ones[...] = jnp.where(whose == lax.broadcasted_iota(jnp.int32, (JPC, CHUNK), 0), 1.0, 0.0).astype(BF16)
 
-    def from_chip(side, k, carry):
+    def from_chip(side, at, carry):
+        k = far(at, CHIPS)
         piece = ms.at[side, core, chip]
         n = (4, 16)[side]
         pltpu.make_async_remote_copy(
@@ -515,14 +549,14 @@
         wait_bytes(m_recv.at[side], recv.at[(2, 15)[side]])
         mine = part[side, core, chip] + pair_recv[side, chip] + jnp.sum(m_recv[side].astype(F32), axis=0)
         ms[side, core, chip] = mine.astype(BF16)
-        lax.fori_loop(1, CHIPS, functools.partial(from_chip, side), 0)
+        lax.fori_loop(0, CHIPS - 1, functools.partial(from_chip, side), 0)
         m16[:, side * BLK:(side + 1) * BLK] = mine
 
     pass_on(0)
     wait_bytes(gb_col.at[pl.ds(0, NCOL - 1)], recv.at[3])
     for i in range(16):
         gb_full[core, me_r, i:i + 1, :] = gb_col[core * 16 + i]
-    gather("row", NROW, gb_full.at[core, me_r], send.at[5], recv.at[5])
+    gather_far("row", NROW, gb_full.at[core, me_r], send.at[5], recv.at[5])
     pass_on(1)
 
     wait_bytes(gb_full.at[0, pl.ds(0, NROW - 1)], recv.at[5])
@@ -547,7 +581,7 @@
     cross = gram[pl.ds(pl.multiple_of(core * (BLK // 2), BLK // 2), BLK // 2), BLK:]
     g_piece[:, :SHARE_G, :] = own.reshape(NROW, SHARE_G, BLK)
     g_piece[:, SHARE_G:, :] = cross.reshape(NROW, SHARE_G // 2, BLK)
-    scatter("row", NROW, g_piece, g_recv, send.at[7], recv.at[7])
+    scatter_far("row", NROW, g_piece, g_recv, send.at[7], recv.at[7])
 
     solved, worst_one = second_half(turned[:, :R], turned[:, R:], down_one, across_one)
     inv1[...] = solved
@@ -590,7 +624,7 @@
     lax.fori_loop(0, 2, mode_two, 0)
     wait_bytes(g_recv, recv.at[7])
     g_full[core, me_r] = g_piece[me_r] + jnp.sum(g_recv[...], axis=0)
-    gather("row", NROW, g_full.at[core, me_r], send.at[8], recv.at[8])
+    gather_far("row", NROW, g_full.at[core, me_r], send.at[8], recv.at[8])
     lax.fori_loop(2, 4, mode_two, 0)
     wait_bytes(g_recv, recv.at[8])
     to_mate(g_full.at[core], g_full.at[core], 9)
@@ -615,7 +649,8 @@
     raw = dot_hi(m2, inv2)
     sq_piece[...] = jnp.sum(raw * raw, axis=0, keepdims=True)
 
-    def to_plane(k, carry):
+    def to_plane(at, carry):
+        k = far(at, PLANE)
         row, col = in_plane(k)
         pltpu.make_async_remote_copy(
             src_ref=sq_piece, dst_ref=sq_col.at[k - 1], send_sem=send.at[11], recv_sem=recv.at[11],
@@ -623,18 +658,19 @@
         ).start()
         return carry
 
-    lax.fori_loop(1, PLANE, to_plane, 0)
+    lax.fori_loop(0, PLANE - 1, to_plane, 0)
     wait_bytes(sq_col, recv.at[11])
     sq_all[...] = sq_piece[...] + jnp.sum(sq_col[...], axis=0)
 
-    def to_planes(k, carry):
+    def to_planes(at, carry):
+        k = far(at, NCOL // 4)
         pltpu.make_async_remote_copy(
             src_ref=sq_all, dst_ref=sq_row.at[k - 1], send_sem=send.at[12], recv_sem=recv.at[12],
             device_id={"col": lax.rem(me_c + k * 4, NCOL)}, device_id_type=MESH,
         ).start()
         return carry
 
-    lax.fori_loop(1, NCOL // 4, to_planes, 0)
+    lax.fori_loop(0, NCOL // 4 - 1, to_planes, 0)
     wait_bytes(gb_recv, send.at[0])
     for side in range(2):
         wait_bytes(pair_recv.at[side], send.at[(1, 14)[side]])

time: 144 us -> 142 us (0.986)
  no operation moved by 1% of the time
where the time goes in v7:
time: 142 us
  Pallas kernels  139 us (98%)
  between operations  2.07 us (1%)
    pallas_call x1, Pallas kernels, body(): pl.pallas_call(kernel_m, name='sweep', out_shape=(shape((SHARE_A, R)), sh...  55.5 us
    pallas_call x1, Pallas kernels, three_kernels(): pl.pallas_call(kernel_a, name='mode_one', out_shape=(shape((R, R)), shape...  37.2 us
    pallas_call x1, Pallas kernels, three_kernels(): pl.pallas_call(kernel_c, name='mode_two', out_shape=shape((SHARE_B, R)),...  25.4 us
    pallas_call x1, Pallas kernels, three_kernels(): pl.pallas_call(kernel_b, name='solve_two', out_shape=(shape((SHARE_A, R))...  20.5 us

profile of v7, /device:TPU:1, one launch (start us, length us, event | category | flops | bytes accessed | tf_op | source)
XLA Modules:
  0.0 142.3 jit_solution(1148329849975135510)
XLA Ops:
  0.6 0.0 copy-start
  0.6 0.0 copy-start.1
  0.7 0.0 copy-start.2
  1.4 55.5 %sweep.1 = (f32[16,256]{1,0:T(8,128)S(1)}, f32[32,256]{1,0:T(8,128)S(1)}, f32[1,1]{1,0:T(1,128)}) custom-call(s32[1,4]{1,0:T(1,128)} %bitcast.5, s32[1,1]{1,0:T(1,128)S(6)} %copy.15.cnt, bf16[512,8192]{1,0:T(8,128)(2,1)} %bitcast.3, f32[256,256]{1,0:T(8,128)} %b_ref.1, f32[64,256]{1,0:T(8,128)} %c_ref.1), custom_call_target="tpu_custom_call" | custom-call | tf_op jit(solution)/shard_map/sweep/pallas_call | solution.py:749
  57.5 0.0 copy-done
  57.6 0.0 copy-done.1
  57.6 0.0 copy-done.2
  57.6 83.5 %conditional.1 = ((f32[16,256]{1,0:T(8,128)S(1)}, f32[32,256]{1,0:T(8,128)S(1)})) conditional(s32[]{:T(128)} %bitcast.2, (s32[1,4]{1,0:T(1,128)S(1)}, s32[1,1]{1,0:T(1,128)}, bf16[512,8192]{1,0:T(8,128)(2,1)}, f32[256,256]{1,0:T(8,128)S(1)}, f32[64,256]{1,0:T(8,128)S(1)}) %tuple.27, (f32[16,256]{1,0:T(8,128)S(1)}, f32[32,256]{1,0:T(8,128)S(1)}) %tuple.15), branch_computations={%region_0.0_spmd, %region_1.0_spmd} | conditional | bytes 24 | solution.py:770
  57.8 37.2 %mode_one.1 = (f32[256,256]{1,0:T(8,128)}, f32[16,256]{1,0:T(8,128)}, bf16[512,256]{1,0:T(8,128)(2,1)}, f32[256,256]{1,0:T(8,128)}) custom-call(s32[1,4]{1,0:T(1,128)S(1)} %get-tuple-element.14.pos, s32[1,1]{1,0:T(1,128)} %get-tuple-element.15.cnt, bf16[512,8192]{1,0:T(8,128)(2,1)} %get-tuple-element.17.x_hbm, f32[256,256]{1,0:T(8,128)S(1)} %get-tuple-element.18.b_ref, ...), custom_call_target="tpu_custom_call" | custom-call | tf_op jit(solution)/shard_map/cond/branch_0_fun/mode_one/pallas_call | solution.py:705
  95.0 20.5 %solve_two.1 = (f32[16,256]{1,0:T(8,128)S(1)}, bf16[512,512]{1,0:T(8,128)(2,1)}, f32[256,256]{1,0:T(8,128)}) custom-call(s32[1,4]{1,0:T(1,128)S(1)} %get-tuple-element.14.pos, s32[1,1]{1,0:T(1,128)} %get-tuple-element.15.cnt, f32[64,256]{1,0:T(8,128)S(1)} %get-tuple-element.16.c_ref, f32[256,256]{1,0:T(8,128)} %get-tuple-element.19.gb_ref, ...), custom_call_target="tpu_custom_call" | custom-call | tf_op jit(solution)/shard_map/cond/branch_0_fun/solve_two/pallas_call | solution.py:721
  115.4 25.4 %mode_two.1 = f32[32,256]{1,0:T(8,128)S(1)} custom-call(bf16[512,8192]{1,0:T(8,128)(2,1)} %get-tuple-element.17.x_hbm, f32[64,256]{1,0:T(8,128)S(1)} %get-tuple-element.16.c_ref, bf16[512,512]{1,0:T(8,128)(2,1)} %get-tuple-element.24.lhs, f32[256,256]{1,0:T(8,128)} %get-tuple-element.25.inv_ref), custom_call_target="tpu_custom_call" | custom-call | tf_op jit(solution)/shard_map/cond/branch_0_fun/mode_two/pallas_call | solution.py:729
  141.1 0.6 copy.16
  141.7 0.6 copy.17
Async XLA Ops:
  0.6 56.9 %copy-start = (f32[64,256]{1,0:T(8,128)S(1)}, f32[64,256]{1,0:T(8,128)}, u32[]{:S(2)}) copy-start(f32[64,256]{1,0:T(8,128)} %c_ref.1) | copy-start | bytes 196612
  0.6 56.9 %copy-start.1 = (f32[256,256]{1,0:T(8,128)S(1)}, f32[256,256]{1,0:T(8,128)}, u32[]{:S(2)}) copy-start(f32[256,256]{1,0:T(8,128)} %b_ref.1) | copy-start | bytes 786436
  0.7 56.9 %copy-start.2 = (s32[4,1]{0,1:T(1,128)S(1)}, s32[4,1]{0,1:T(1,128)}, u32[]{:S(2)}) copy-start(s32[4,1]{0,1:T(1,128)} %param.10) | copy-start | bytes 52
